TPU v7x, 512 devices: a whole 4x8x8 slice. The times are simulated.
512 devices in a mesh: sub: 4 (over z_lo), row: 16 (over z_hi, x, core), col: 8 (over y).
Axes of the slice: x: 4, y: 8, z: 8 (z_hi: 2, z_lo: 4; z = z_hi * 4 + z_lo), core: 2. Of those that a mesh axis runs over, the one named last changes fastest.
Arguments:
- child_update: bfloat16 [32768, 8192], P(('sub', 'row'), 'col'), may hold values from -2.8 to 2.8, as said below
- parent_front: bfloat16 [16384, 16384], P('row', ('sub', 'col')), may hold values from -2.8 to 256, as said below
- tile_map: int32 [4, 64], replicated, may hold values from -1 to 127, as said below
Outputs:
- front_out: float32 [16384, 16384], P('row', ('sub', 'col'))
Inputs may be any that keep to these rules, and one draw needn't show every extreme that they name: Live tiles of a child come first, a whole multiple of 16 of them, at least max(1, 2) * 16; then -1. At least one child has all 64 tiles live. Within one child the parent tiles are distinct, and (tile_map[s, j] // 4) % 16 == j % 16 for every live j. `child_update`: each child's update, in logical order, is a symmetric matrix. `parent_front`: symmetric in logical order, with diagonal entries between 64 and 256; the assembled leading 4 x 4 tiles are positive definite.
All inputs are finite; a program needn't handle non-finite values.
Results may differ from a plain program's by a relative error of at most 0.0008.
Values may be sent and summed in bfloat16 or wider, within the bound.
A program may use at most 64 MiB of HBM per device.

v0:
```python
import jax
import jax.numpy as jnp
from jax import lax
from jax.sharding import PartitionSpec as P

TILE = 128
PANEL = 4


precise = lax.Precision.HIGHEST


def from_root(x, axis, root):
    mine = lax.axis_index(axis) == root
    return lax.psum(jnp.where(mine, x, jnp.zeros_like(x)), axis)


def body(child_update, parent_front, tile_map):
    tile_len = TILE
    panel_tiles = PANEL
    panel_width = panel_tiles * tile_len
    sub_count = lax.axis_size("sub")
    row_count = lax.axis_size("row")
    col_count = lax.axis_size("col")
    sub_id = lax.axis_index("sub")
    row_id = lax.axis_index("row")
    col_id = lax.axis_index("col")
    block_id = sub_id * col_count + col_id
    child_rows = child_update.shape[0] // tile_len
    child_cols = child_update.shape[1] // tile_len
    front_rows = parent_front.shape[0] // tile_len
    own_map = lax.dynamic_index_in_dim(tile_map, sub_id, 0, keepdims=False)
    own_cols = lax.dynamic_index_in_dim(
        own_map.reshape(child_cols, col_count), col_id, 1, keepdims=False
    )
    live_cols = own_cols >= 0
    destination = jnp.floor_divide(jnp.floor_divide(own_cols, panel_tiles), col_count)
    slot_index = jnp.remainder(own_cols, panel_tiles)
    dest_hit = destination[None, :] == jnp.arange(sub_count, dtype=jnp.int32)[:, None]
    slot_hit = slot_index[None, :] == jnp.arange(panel_tiles, dtype=jnp.int32)[:, None]
    select = (live_cols[None, None, :] & dest_hit[:, None, :] & slot_hit[None, :, :]).astype(
        jnp.bfloat16
    )
    column_slabs = child_update.reshape(child_rows * tile_len, child_cols, tile_len)
    payload = jnp.einsum(
        "dqk,rky->dqry", select, column_slabs, preferred_element_type=jnp.float32
    ).astype(jnp.bfloat16)
    maps_rows = lax.dynamic_index_in_dim(
        tile_map.reshape(sub_count, child_rows, row_count), row_id, 2, keepdims=False
    )
    local_row = jnp.floor_divide(
        jnp.floor_divide(maps_rows, panel_tiles), row_count
    ) * panel_tiles + jnp.remainder(maps_rows, panel_tiles)
    row_hit = (maps_rows[:, :, None] >= 0) & (
        local_row[:, :, None] == jnp.arange(front_rows, dtype=jnp.int32)[None, None, :]
    )
    place_row = row_hit.astype(jnp.bfloat16)
    arrived = lax.all_to_all(payload, "sub", split_axis=0, concat_axis=0, tiled=True)
    slot_count = arrived.shape[1]
    grid = arrived.reshape(sub_count, slot_count, child_rows, tile_len, tile_len)
    spread = jnp.einsum("ska,sqkyx->ayqx", place_row, grid, preferred_element_type=jnp.float32)
    placed = spread.reshape(front_rows * tile_len, slot_count * tile_len)
    front_local = parent_front.astype(jnp.float32) + placed
    top_block = from_root(front_local[:panel_width].astype(jnp.bfloat16), "row", 0).astype(
        jnp.float32
    )
    panel_rows, leading = (
        from_root(front_local.astype(jnp.bfloat16), ("sub", "col"), 0).astype(front_local.dtype),
        from_root(top_block.astype(jnp.bfloat16), ("sub", "col"), 0).astype(top_block.dtype),
    )
    lower_factor = jnp.tril(jnp.linalg.cholesky(leading))
    identity = jnp.eye(panel_width, dtype=jnp.float32)
    inverse = jax.scipy.linalg.solve_triangular(lower_factor, identity, lower=True)
    factor_rows = jnp.dot(
        panel_rows, inverse.T, precision=precise, preferred_element_type=jnp.float32
    )
    head_rows = jnp.where(row_id == 0, lower_factor, factor_rows[:panel_width])
    factor_rows = jnp.concatenate([head_rows, factor_rows[panel_width:]], axis=0)
    source_row = jnp.remainder(block_id, row_count)
    first_row = jnp.floor_divide(block_id, row_count) * panel_width
    factor_piece = lax.dynamic_slice_in_dim(factor_rows, first_row, panel_width, 0)
    column_side = from_root(factor_piece.astype(jnp.bfloat16), "row", source_row).astype(
        factor_piece.dtype
    )
    update = jnp.dot(
        factor_rows, column_side.T, precision=precise, preferred_element_type=jnp.float32
    )
    keep_rows = (jnp.arange(front_rows * tile_len) >= panel_width) | (row_id != 0)
    trailing = front_local - jnp.where(keep_rows[:, None], update, 0.0)
    return jnp.where(block_id == 0, factor_rows, trailing)


def solution(mesh):
    in_specs = (P(("sub", "row"), "col"), P("row", ("sub", "col")), P())
    out_specs = P("row", ("sub", "col"))
    return jax.shard_map(body, mesh=mesh, in_specs=in_specs, out_specs=out_specs, check_vma=False)
```

profile of v0, /device:TPU:449, one launch (start us, length us, event | category | flops | bytes accessed | tf_op | source)
XLA Modules:
  0.0 931.0 jit_solution(14643982582038537792)
XLA Ops:
  6.5 0.7 fusion.65
  7.5 1.5 copy.51
  9.1 2.0 convolution_convert_fusion
  11.1 4.7 all-to-all-start
  16.3 1.5 copy.23
  17.8 43.2 %all-to-all-done = bf16[4,4,512,128]{3,1,2,0:T(4,128)(2,1)S(1)} async-done(((bf16[4,4,512,128]{3,1,2,0:T(4,128)(2,1)}), bf16[4,4,512,128]{3,1,2,0:T(4,128)(2,1)S(1)}, u32[]{:S(2)}, u32[]{:S(2)}) %all-to-all-start) | async-done | bytes 2097184 | tf_op jit(solution)/shard_map/all_to_all | solution.py:58
  61.0 5.0 fusion.3
  66.0 2.0 copy.28
  68.1 1.7 broadcast_select_fusion
  69.8 0.8 slice_select_fusion.1
  70.7 184.0 %all-reduce.6.cloned.1.call-done = bf16[512,512]{0,1:T(8,128)(2,1)} async-done(((bf16[512,512]{0,1:T(8,128)(2,1)}), bf16[512,512]{0,1:T(8,128)(2,1)}) %all-reduce.6.cloned.1.call-update) | async-done | bytes 524304 | tf_op jit(solution)/shard_map/psum | solution.py:15
  254.8 0.8 broadcast_select_fusion.1
  255.9 0.8 iota_compare_fusion
  256.6 1.2 fusion.28
  257.8 284.4 %all-reduce.10.cloned.1.call-done = (bf16[512,512]{0,1:T(8,128)(2,1)}, bf16[1024,512]{0,1:T(8,128)(2,1)}) async-done(((bf16[512,512]{0,1:T(8,128)(2,1)}, bf16[1024,512]{0,1:T(8,128)(2,1)}), (bf16[512,512]{0,1:T(8,128)(2,1)}, bf16[1024,512]{0,1:T(8,128)(2,1)})) %all-reduce.10.cloned.1.call-update) | async-done | bytes 1572880 | tf_op jit(solution)/shard_map/psum | solution.py:15
  542.2 1.3 copy.29
  543.5 1.2 fusion.17
  544.7 1.0 copy-done.4
  545.7 11.7 %cholesky.104 = f32[128,128]{1,0:T(8,128)S(1)} custom-call(f32[128,128]{1,0:T(8,128)S(1)} %cholesky.266), custom_call_target="Cholesky" | custom-call | tf_op jit(solution)/shard_map/jit(cholesky)/cholesky | solution.py:71
  557.4 0.7 copy.30
  558.2 9.8 %custom-call.31 = f32[1,128,128]{1,2,0:T(8,128)S(1)} custom-call(f32[1,128,128]{2,1,0:T(8,128)S(1)} %get-tuple-element.42), custom_call_target="InvertDiagBlocksLowerTriangular" | custom-call | tf_op jit(solution)/shard_map/jit(cholesky)/cholesky | solution.py:71
  568.0 1.2 fusion.34
  569.3 1.3 convolution_subtract_fusion.3
  570.6 11.7 %cholesky.217 = f32[128,128]{1,0:T(8,128)S(1)} custom-call(f32[128,128]{1,0:T(8,128)S(1)} %cholesky.270), custom_call_target="Cholesky" | custom-call | tf_op jit(solution)/shard_map/jit(cholesky)/cholesky | solution.py:71
  582.3 0.7 copy.32
  583.1 10.6 %custom-call.32 = f32[1,128,128]{1,2,0:T(8,128)} custom-call(f32[1,128,128]{2,1,0:T(8,128)S(1)} %get-tuple-element.40), custom_call_target="InvertDiagBlocksLowerTriangular" | custom-call | tf_op jit(solution)/shard_map/jit(cholesky)/cholesky | solution.py:71
  593.7 1.0 cholesky.224
  594.7 0.8 constant_dynamic-update-slice_fusion.3
  595.5 1.2 convolution_dynamic-update-slice_fusion
  596.7 1.5 convolution_subtract_fusion.4
  598.2 11.7 %cholesky.238 = f32[128,128]{1,0:T(8,128)S(1)} custom-call(f32[128,128]{1,0:T(8,128)S(1)} %cholesky.275), custom_call_target="Cholesky" | custom-call | tf_op jit(solution)/shard_map/jit(cholesky)/cholesky | solution.py:71
  610.1 9.8 %custom-call.33 = f32[1,128,128]{1,2,0:T(8,128)S(1)} custom-call(f32[1,128,128]{2,1,0:T(8,128)S(1)} %get-tuple-element.38), custom_call_target="InvertDiagBlocksLowerTriangular" | custom-call | tf_op jit(solution)/shard_map/jit(cholesky)/cholesky | solution.py:71
  620.2 1.3 convolution_subtract_fusion.5
  621.5 11.9 %cholesky.255 = f32[128,128]{1,0:T(8,128)S(1)} custom-call(f32[128,128]{1,0:T(8,128)S(1)} %convolution_subtract_fusion.5), custom_call_target="Cholesky" | custom-call | tf_op jit(solution)/shard_map/jit(cholesky)/cholesky | solution.py:71
  633.6 0.7 compare_reduce_fusion.3
  634.4 0.7 compare_reduce_fusion.2
  635.1 0.7 compare_reduce_fusion.1
  635.8 0.6 compare_reduce_fusion
  638.9 1.1 fusion.18
  640.0 14.7 %while.1 = (s32[]{:T(128)}, f32[512,512]{0,1:T(8,128)}, s32[4,2]{0,1:T(2,128)S(1)}, f32[4,128,128]{2,1,0:T(8,128)}, s32[]{:T(128)}) while((s32[]{:T(128)}, f32[512,512]{0,1:T(8,128)}, s32[4,2]{0,1:T(2,128)S(1)}, f32[4,128,128]{2,1,0:T(8,128)}, s32[]{:T(128)}) %tuple.28), condition=%wide.while_cond, body=%wide.while_body.sunk | while | flops 2 | bytes 393329 | solution.py:73
  640.1 0.6 fusion.81
  640.7 2.3 dynamic-slice.7
  643.1 0.6 bitcast_dynamic-update-slice_fusion.2
  643.8 0.6 fusion.81
  644.4 2.3 dynamic-slice.7
  646.8 0.6 bitcast_dynamic-update-slice_fusion.2
  647.5 0.6 fusion.81
  648.1 2.3 dynamic-slice.7
  650.5 0.6 bitcast_dynamic-update-slice_fusion.2
  651.2 0.6 fusion.81
  651.7 2.2 dynamic-slice.7
  654.1 0.6 bitcast_dynamic-update-slice_fusion.2
  654.7 40.1 %custom-call.34 = f32[4,128,128]{1,2,0:T(8,128)S(1)} custom-call(f32[4,128,128]{2,1,0:T(8,128)} %get-tuple-element.12), custom_call_target="InvertDiagBlocksLowerTriangular" | custom-call | tf_op jit(solution)/shard_map/jit(_solve_triangular)/triangular_solve | solution.py:73
  694.8 1.1 fusion.30
  695.9 1.4 convolution_subtract_fusion.1
  697.8 1.5 convolution_subtract_fusion
  699.3 0.4 fusion.40
  699.7 1.7 convolution_subtract_fusion.2
  701.9 1.8 fusion.9
  704.0 1.0 copy-done
  705.0 1.1 fusion.24
  706.1 209.4 %all-reduce.8.cloned.1.call-done = bf16[512,512]{0,1:T(8,128)(2,1)} async-done(((bf16[512,512]{0,1:T(8,128)(2,1)}), bf16[512,512]{0,1:T(8,128)(2,1)}) %all-reduce.8.cloned.1.call-update) | async-done | bytes 524304 | tf_op jit(solution)/shard_map/psum | solution.py:15
  915.5 5.6 subtract_select_fusion
  921.1 2.9 copy.41
  (59 shorter events, 3.7 us)
Async XLA Ops:
  11.1 4.7 copy-start.6
  11.1 49.9 %all-to-all-start = ((bf16[4,4,512,128]{3,1,2,0:T(4,128)(2,1)}), bf16[4,4,512,128]{3,1,2,0:T(4,128)(2,1)S(1)}, u32[]{:S(2)}, u32[]{:S(2)}) async-start(bf16[4,4,512,128]{3,1,2,0:T(4,128)(2,1)} %convolution_convert_fusion), calls=%async_computation | async-start | bytes 4194304 | tf_op jit(solution)/shard_map/all_to_all | solution.py:58
  15.8 239.0 %all-reduce.6.cloned.1.call-start = ((), (), s32[]{:S(2)}) async-start(), calls=%async_computation.1 | async-start | bytes 1048576 | tf_op jit(solution)/shard_map/psum | solution.py:15
  17.8 50.3 %copy-start.3 = (bf16[1024,512]{0,1:T(8,128)(2,1)}, bf16[1024,512]{0,1:T(8,128)(2,1)S(1)}, u32[]{:S(2)}) copy-start(bf16[1024,512]{0,1:T(8,128)(2,1)S(1)} %copy.23) | copy-start | bytes 3145732
  70.7 471.6 %all-reduce.10.cloned.1.call-start = ((), (), s32[]{:S(2)}) async-start(), calls=%async_computation.3 | async-start | bytes 3145728 | tf_op jit(solution)/shard_map/psum | solution.py:15
  255.6 659.9 %all-reduce.8.cloned.1.call-start = ((), (), s32[]{:S(2)}) async-start(), calls=%async_computation.2 | async-start | bytes 1048576 | tf_op jit(solution)/shard_map/psum | solution.py:15
  544.7 1.0 copy-start.4
  633.6 6.4 copy-start.1
  697.4 4.5 copy-start.5
  701.9 1.8 copy-start.2
  704.0 1.0 copy-start
Sparse Core Ops, SparseCore 0:
  70.8 183.9 all-reduce.5
  257.7 284.4 all-reduce.9
  706.2 209.2 all-reduce.7
where the time goes:
time: 946 us; the launch traced here: 931 us
  waiting for transfers between devices  721 us (76%)
  other arithmetic  129 us (14%)
  local copies, waits for them, and re-layouts  30.8 us (3%)
  matrix products  28.2 us (3%)
  between operations  16.5 us (2%)
    psum x3, waiting for transfers between devices, from_root(): return lax.psum(jnp.where(mine, x, jnp.zeros_like(x)), axis)  678 us
    another operation x15, other arithmetic, body(): lower_factor = jnp.tril(jnp.linalg.cholesky(leading))  80.2 us
    all_to_all x1, waiting for transfers between devices, body(): lax.all_to_all(payload, 'sub', split_axis=0, concat_axis=0, tiled=True)  43.2 us
    another operation x3, other arithmetic, body(): jax.scipy.linalg.solve_triangular(lower_factor, identity, lower=True)  41.2 us
  transfers between devices with their start and end apart: 4, of which 4 were waited for; matrix products, arithmetic and copies ran while one was open for 0% of the time, Pallas kernels for 0%

commit v1 on v0

v1 whole, which is shorter than its diff:
```python
import functools

import jax
import jax.numpy as jnp
from jax import lax
from jax.experimental import pallas as pl
from jax.experimental.pallas import tpu as pltpu
from jax.sharding import PartitionSpec as P

TILE = 128
PANEL = 4
WIDTH = TILE * PANEL
MESH = pl.DeviceIdType.MESH
GROUP = 8
PIECE = WIDTH // GROUP


def remote(src, dst, send_sem, recv_sem, device):
    return pltpu.make_async_remote_copy(
        src_ref=src,
        dst_ref=dst,
        send_sem=send_sem,
        recv_sem=recv_sem,
        device_id=device,
        device_id_type=MESH,
    )


def each(count, skip, fn):
    def step(i, _):
        @pl.when(i != skip)
        def _():
            fn(i)

        return 0

    lax.fori_loop(0, count, step, 0)


def spread_kernel(
    n_sub,
    n_row,
    n_col,
    front,
    panel,
    top,
    lead,
    local_sem,
    top_send,
    top_cross,
    top_gather,
    top_recv,
    panel_send,
    panel_first,
    panel_recv,
    lead_sub,
    lead_col,
    lead_gather,
    lead_recv,
):
    s, r, c = lax.axis_index("sub"), lax.axis_index("row"), lax.axis_index("col")
    plane = n_sub * n_col
    p = s * n_col + c
    half, i = r // GROUP, r % GROUP
    depth = front.shape[0] // plane

    def at_plane(q):
        return (q // n_col, r, q % n_col)

    def at_group(j):
        return (s, half * GROUP + j, c)

    def top_piece(j):
        return top.at[pl.ds(pl.multiple_of(j * PIECE, PIECE), PIECE)]

    def lead_piece(j):
        return lead.at[pl.ds(pl.multiple_of(j * PIECE, PIECE), PIECE)]

    def panel_piece(q):
        return panel.at[pl.ds(pl.multiple_of(q * depth, depth), depth)]

    def front_piece(q):
        return front.at[pl.ds(pl.multiple_of(q * depth, depth), depth)]

    def front_top(j):
        return front.at[pl.ds(pl.multiple_of(j * PIECE, PIECE), PIECE)]

    barrier = pltpu.get_barrier_semaphore()
    across = (s, (1 - half) * GROUP + i, c)

    def greet(device):
        pl.semaphore_signal(barrier, inc=1, device_id=device, device_id_type=MESH)

    each(plane, p, lambda q: greet(at_plane(q)))
    each(GROUP, i, lambda j: greet(at_group(j)))
    greet(across)
    pl.semaphore_wait(barrier, plane - 1 + GROUP - 1 + 1)

    top_scatter = lambda j: remote(
        front_top(j), top_piece(j), top_send.at[j], top_recv.at[j], at_group(j)
    )
    panel_scatter = lambda q: remote(
        front_piece(q), panel_piece(q), panel_send.at[q], panel_recv.at[q], at_plane(q)
    )
    panel_zero = lambda q: remote(
        front_piece(0), panel_piece(0), panel_first.at[q], panel_recv.at[0], at_plane(q)
    )
    top_over = remote(top_piece(i), top_piece(i), top_cross, top_recv.at[i], across)
    top_share = lambda j: remote(
        top_piece(i), top_piece(i), top_gather.at[j], top_recv.at[i], at_group(j)
    )
    panel_share = lambda q: remote(
        panel_piece(p), panel_piece(p), panel_send.at[q], panel_recv.at[p], at_plane(q)
    )
    lead_down = lambda k: remote(
        top_piece(i), lead_piece(i), lead_sub.at[k], lead_recv.at[i], (k, r, 0)
    )
    lead_along = lambda k: remote(
        top_piece(i), lead_piece(i), lead_col.at[k], lead_recv.at[i], (s, r, k)
    )
    lead_forward = lambda k: remote(
        lead_piece(i), lead_piece(i), lead_col.at[k], lead_recv.at[i], (s, r, k)
    )
    lead_share = lambda j: remote(
        lead_piece(i), lead_piece(i), lead_gather.at[j], lead_recv.at[i], at_group(j)
    )
    own_top = pltpu.make_async_copy(front.at[pl.ds(0, WIDTH)], top, local_sem.at[0])
    own_panel = pltpu.make_async_copy(front, panel, local_sem.at[1])
    own_lead = pltpu.make_async_copy(top, lead, local_sem.at[2])

    def arrived(piece, sem):
        pltpu.make_async_copy(piece, piece, sem).wait()

    @pl.when(r == 0)
    def _():
        own_top.start()
        each(GROUP, 0, lambda j: top_scatter(j).start())

    @pl.when(p == 0)
    def _():
        own_panel.start()
        each(plane, 0, lambda q: panel_scatter(q).start())
        each(plane, 0, lambda q: panel_zero(q).start())

    @pl.when(r == 0)
    def _():
        own_top.wait()

    @pl.when(r != 0)
    def _():
        arrived(top_piece(i), top_recv.at[i])

    @pl.when(p == 0)
    def _():
        each(n_sub, 0, lambda k: lead_down(k).start())
        each(n_col, 0, lambda k: lead_along(k).start())

    @pl.when(half == 0)
    def _():
        top_over.start()
        each(GROUP, i, lambda j: pl.when(j != 0)(lambda: top_share(j).start()))

    @pl.when(half != 0)
    def _():
        each(GROUP, i, lambda j: top_share(j).start())

    @pl.when(p != 0)
    def _():
        arrived(panel_piece(p), panel_recv.at[p])
        each(plane, p, lambda q: pl.when(q != 0)(lambda: panel_share(q).start()))
        arrived(lead_piece(i), lead_recv.at[i])

        @pl.when(c == 0)
        def _():
            each(n_col, 0, lambda k: lead_forward(k).start())

        each(GROUP, i, lambda j: lead_share(j).start())

    @pl.when(r != 0)
    def _():
        each(GROUP, i, lambda j: arrived(top_piece(j), top_recv.at[j]))

    @pl.when(p == 0)
    def _():
        own_lead.start()

    @pl.when(p != 0)
    def _():
        each(GROUP, i, lambda j: arrived(lead_piece(j), lead_recv.at[j]))
        each(plane, p, lambda q: arrived(panel_piece(q), panel_recv.at[q]))

    @pl.when(r == 0)
    def _():
        each(GROUP, 0, lambda j: top_scatter(j).wait_send())

    @pl.when(half == 0)
    def _():
        top_over.wait_send()
        each(GROUP, i, lambda j: pl.when(j != 0)(lambda: top_share(j).wait_send()))

    @pl.when(half != 0)
    def _():
        each(GROUP, i, lambda j: top_share(j).wait_send())

    @pl.when(p == 0)
    def _():
        own_panel.wait()
        own_lead.wait()
        each(plane, 0, lambda q: panel_scatter(q).wait_send())
        each(plane, 0, lambda q: panel_zero(q).wait_send())
        each(n_sub, 0, lambda k: lead_down(k).wait_send())
        each(n_col, 0, lambda k: lead_along(k).wait_send())

    @pl.when(p != 0)
    def _():
        each(plane, p, lambda q: pl.when(q != 0)(lambda: panel_share(q).wait_send()))

        @pl.when(c == 0)
        def _():
            each(n_col, 0, lambda k: lead_forward(k).wait_send())

        each(GROUP, i, lambda j: lead_share(j).wait_send())


def spread_panels(front16, n_sub, n_row, n_col):
    rows, width = front16.shape
    vmem = pl.BlockSpec(memory_space=pltpu.VMEM)
    dma = pltpu.SemaphoreType.DMA
    plane = n_sub * n_col
    return pl.pallas_call(
        functools.partial(spread_kernel, n_sub, n_row, n_col),
        out_shape=(
            jax.ShapeDtypeStruct((rows, width), jnp.bfloat16),
            jax.ShapeDtypeStruct((WIDTH, width), jnp.bfloat16),
            jax.ShapeDtypeStruct((WIDTH, width), jnp.bfloat16),
        ),
        in_specs=[vmem],
        out_specs=(vmem, vmem, vmem),
        scratch_shapes=[
            dma((3,)),
            dma((GROUP,)),
            dma(()),
            dma((GROUP,)),
            dma((GROUP,)),
            dma((plane,)),
            dma((plane,)),
            dma((plane,)),
            dma((n_sub,)),
            dma((n_col,)),
            dma((GROUP,)),
            dma((GROUP,)),
        ],
        compiler_params=pltpu.CompilerParams(collective_id=0, has_side_effects=True),
        name="spread_panels",
    )(front16)


def invert_block(load_group, store_rows):
    sub = 8
    groups = TILE // sub
    lane = lax.broadcasted_iota(jnp.int32, (sub, TILE), 1)
    line = lax.broadcasted_iota(jnp.int32, (sub, TILE), 0)
    a = [load_group(g) for g in range(groups)]
    m = [jnp.where(lane == line + sub * g, 1.0, 0.0).astype(jnp.float32) for g in range(groups)]
    b = 4
    for j0 in range(0, TILE, b):
        g0, i0 = divmod(j0, sub)
        rows_a = [jnp.broadcast_to(a[g0][i0 + k : i0 + k + 1, :], (sub, TILE)) for k in range(b)]
        rows_m = [jnp.broadcast_to(m[g0][i0 + k : i0 + k + 1, :], (sub, TILE)) for k in range(b)]
        piv = [
            [
                jnp.broadcast_to(rows_a[l][:, j0 + k : j0 + k + 1], (sub, TILE))
                for k in range(l + 1)
            ]
            for l in range(b)
        ]
        low = [[None] * b for _ in range(b)]
        inv_diag = [None] * b
        for k in range(b):
            d = piv[k][k]
            for q in range(k):
                d = d - low[k][q] * low[k][q]
            inv_diag[k] = lax.rsqrt(d)
            for l in range(k + 1, b):
                v = piv[l][k]
                for q in range(k):
                    v = v - low[l][q] * low[k][q]
                low[l][k] = v * inv_diag[k]

        def solve(rows):
            out = []
            for l in range(b):
                v = rows[l]
                for q in range(l):
                    v = v - low[l][q] * out[q]
                out.append(v * inv_diag[l])
            return out

        def solve_back(rows):
            out = [None] * b
            for l in reversed(range(b)):
                v = rows[l]
                for q in range(l + 1, b):
                    v = v - low[q][l] * out[q]
                out[l] = v * inv_diag[l]
            return out

        x = solve(rows_m)
        store_rows(j0, x)
        if j0 + b == TILE:
            break
        va, vm = solve_back(solve(rows_a)), solve_back(x)
        first = (j0 + b) // sub
        for g in range(first, groups):
            for k in range(b):
                col = jnp.broadcast_to(a[g][:, j0 + k : j0 + k + 1], (sub, TILE))
                if g == g0:
                    col = jnp.where(line >= i0 + b, col, 0.0)
                if k == 0:
                    da, dm = col * va[0], col * vm[0]
                else:
                    da, dm = da + col * va[k], dm + col * vm[k]
            a[g], m[g] = a[g] - da, m[g] - dm


def split(x):
    high = x.astype(jnp.bfloat16)
    return high, (x - high.astype(jnp.float32)).astype(jnp.bfloat16)


def mul(x, y, transposed=False):
    dims = (((1,), (1 if transposed else 0,)), ((), ()))
    return lax.dot_general(x, y, dims, preferred_element_type=jnp.float32)


def mul3(x, y, transposed=False):
    xh, xl = split(x)
    yh, yl = split(y)
    return mul(xh, yh, transposed) + (mul(xh, yl, transposed) + mul(xl, yh, transposed))


def factor_kernel(lead, top, panel, front, out, work, inverse, lower, block_inv, right):
    row_id = lax.axis_index("row")
    block_id = lax.axis_index("sub") * lax.axis_size("col") + lax.axis_index("col")
    width = WIDTH
    work[...] = lead[...].astype(jnp.float32)
    row_of = lax.broadcasted_iota(jnp.int32, (width, width), 0)
    col_of = lax.broadcasted_iota(jnp.int32, (width, width), 1)
    inverse[...] = jnp.where(row_of == col_of, 1.0, 0.0).astype(jnp.float32)
    lower[...] = jnp.zeros_like(lower)

    for kb in range(PANEL):
        o = kb * TILE

        def load_group(g):
            return work[o + 8 * g : o + 8 * g + 8, o : o + TILE]

        def store_rows(j0, x):
            for k in range(len(x)):
                block_inv[j0 + k : j0 + k + 1, :] = x[k][0:1, :]

        invert_block(load_group, store_rows)
        d_inv = block_inv[...]
        rest = width - o - TILE
        diag = mul3(work[o : o + TILE, o : o + TILE], d_inv, True)
        tri = lax.broadcasted_iota(jnp.int32, (TILE, TILE), 0) >= lax.broadcasted_iota(
            jnp.int32, (TILE, TILE), 1
        )
        lower[o : o + TILE, o : o + TILE] = jnp.where(tri, diag, 0.0)
        x_rows = mul3(d_inv, inverse[o : o + TILE, 0 : o + TILE])
        inverse[o : o + TILE, 0 : o + TILE] = x_rows
        if rest:
            below = mul3(work[o + TILE :, o : o + TILE], d_inv, True)
            lower[o + TILE :, o : o + TILE] = below
            work[o + TILE :, o + TILE :] = work[o + TILE :, o + TILE :] - mul3(below, below, True)
            inverse[o + TILE :, 0 : o + TILE] = inverse[o + TILE :, 0 : o + TILE] - mul3(
                below, x_rows
            )

    inv_high, inv_low = split(inverse[...])
    tops = top[...]
    right[...] = mul(inv_high, tops) + mul(inv_low, tops)
    chunk = 128

    @pl.loop(0, panel.shape[0] // chunk)
    def _(t):
        rows = pl.ds(pl.multiple_of(t * chunk, chunk), chunk)
        a_rows = panel[rows, :]
        xh, xl = split(inverse[...])
        f_rows = mul(a_rows, xh, True) + mul(a_rows, xl, True)
        head = (row_id == 0) & (t < width // chunk)

        @pl.when(block_id == 0)
        def _():
            out[rows, :] = f_rows

            @pl.when(head)
            def _():
                out[rows, :] = lower[rows, :]

        @pl.when(block_id != 0)
        def _():
            @pl.when(head)
            def _():
                out[rows, :] = front[rows, :]

            @pl.when(jnp.logical_not(head))
            def _():
                out[rows, :] = front[rows, :] - mul3(f_rows, right[...])


def factor_and_update(lead, top, panel, front):
    vmem = pl.BlockSpec(memory_space=pltpu.VMEM)
    return pl.pallas_call(
        factor_kernel,
        out_shape=jax.ShapeDtypeStruct(front.shape, jnp.float32),
        in_specs=[vmem] * 4,
        out_specs=vmem,
        scratch_shapes=[
            pltpu.VMEM((WIDTH, WIDTH), jnp.float32),
            pltpu.VMEM((WIDTH, WIDTH), jnp.float32),
            pltpu.VMEM((WIDTH, WIDTH), jnp.float32),
            pltpu.VMEM((TILE, TILE), jnp.float32),
            pltpu.VMEM((WIDTH, WIDTH), jnp.float32),
        ],
        name="factor_and_update",
    )(lead, top, panel, front)


def body(child_update, parent_front, tile_map):
    tile_len = TILE
    panel_tiles = PANEL
    sub_count = lax.axis_size("sub")
    row_count = lax.axis_size("row")
    col_count = lax.axis_size("col")
    sub_id = lax.axis_index("sub")
    row_id = lax.axis_index("row")
    col_id = lax.axis_index("col")
    child_rows = child_update.shape[0] // tile_len
    child_cols = child_update.shape[1] // tile_len
    front_rows = parent_front.shape[0] // tile_len
    own_map = lax.dynamic_index_in_dim(tile_map, sub_id, 0, keepdims=False)
    own_cols = lax.dynamic_index_in_dim(
        own_map.reshape(child_cols, col_count), col_id, 1, keepdims=False
    )
    live_cols = own_cols >= 0
    destination = jnp.floor_divide(jnp.floor_divide(own_cols, panel_tiles), col_count)
    slot_index = jnp.remainder(own_cols, panel_tiles)
    dest_hit = destination[None, :] == jnp.arange(sub_count, dtype=jnp.int32)[:, None]
    slot_hit = slot_index[None, :] == jnp.arange(panel_tiles, dtype=jnp.int32)[:, None]
    select = (live_cols[None, None, :] & dest_hit[:, None, :] & slot_hit[None, :, :]).astype(
        jnp.bfloat16
    )
    column_slabs = child_update.reshape(child_rows * tile_len, child_cols, tile_len)
    payload = jnp.einsum(
        "dqk,rky->dqry", select, column_slabs, preferred_element_type=jnp.float32
    ).astype(jnp.bfloat16)
    maps_rows = lax.dynamic_index_in_dim(
        tile_map.reshape(sub_count, child_rows, row_count), row_id, 2, keepdims=False
    )
    local_row = jnp.floor_divide(
        jnp.floor_divide(maps_rows, panel_tiles), row_count
    ) * panel_tiles + jnp.remainder(maps_rows, panel_tiles)
    row_hit = (maps_rows[:, :, None] >= 0) & (
        local_row[:, :, None] == jnp.arange(front_rows, dtype=jnp.int32)[None, None, :]
    )
    place_row = row_hit.astype(jnp.bfloat16)
    arrived = lax.all_to_all(payload, "sub", split_axis=0, concat_axis=0, tiled=True)
    slot_count = arrived.shape[1]
    grid = arrived.reshape(sub_count, slot_count, child_rows, tile_len, tile_len)
    spread = jnp.einsum("ska,sqkyx->ayqx", place_row, grid, preferred_element_type=jnp.float32)
    placed = spread.reshape(front_rows * tile_len, slot_count * tile_len)
    front_local = parent_front.astype(jnp.float32) + placed
    panel, top, lead = spread_panels(
        front_local.astype(jnp.bfloat16), sub_count, row_count, col_count
    )
    return factor_and_update(lead, top, panel, front_local)


def solution(mesh):
    in_specs = (P(("sub", "row"), "col"), P("row", ("sub", "col")), P())
    out_specs = P("row", ("sub", "col"))
    return jax.shard_map(body, mesh=mesh, in_specs=in_specs, out_specs=out_specs, check_vma=False)
```

time: 946 us -> 173 us (0.18)
  the two profiles are of different devices: /device:TPU:449 before, /device:TPU:481 now
where the time goes in v1:
time: 173 us
  Pallas kernels  111 us (64%)
  waiting for transfers between devices  44.7 us (26%)
  matrix products  5.72 us (3%)
  starting transfers between devices  4.66 us (3%)
  local copies, waits for them, and re-layouts  4.29 us (2%)
  other arithmetic  2.19 us (1%)
    pallas_call x1, Pallas kernels, spread_panels(): pl.pallas_call(functools.partial(spread_kernel, n_sub, n_row, n_col), out...  70.4 us
    all_to_all x1, waiting for transfers between devices, body(): lax.all_to_all(payload, 'sub', split_axis=0, concat_axis=0, tiled=True)  44.7 us
    pallas_call x1, Pallas kernels, factor_and_update(): pl.pallas_call(factor_kernel, out_shape=jax.ShapeDtypeStruct(front.shape,...  40.9 us
    all_to_all x1, starting transfers between devices, body(): lax.all_to_all(payload, 'sub', split_axis=0, concat_axis=0, tiled=True)  4.66 us
    dot_general x1, matrix products, body(): jnp.einsum('ska,sqkyx->ayqx', place_row, grid, preferred_element_type=jnp...  3.69 us
  transfers between devices with their start and end apart: 1, of which 1 were waited for; matrix products, arithmetic and copies ran while one was open for 0% of the time, Pallas kernels for 0%

profile of v1, /device:TPU:481, one launch (start us, length us, event | category | flops | bytes accessed | tf_op | source)
XLA Modules:
  0.0 173.0 jit_solution(16318142321595500874)
XLA Ops:
  0.0 0.7 fusion.21
  0.7 0.1 reshape.138
  0.8 0.2 dynamic-slice_reduce_fusion
  1.0 1.5 copy.18
  2.5 2.0 %convolution_convert_fusion = bf16[4,4,512,128]{3,1,2,0:T(4,128)(2,1)} fusion(bf16[512,8,128,1]{2,1,0,3:T(8,128)(2,1)S(1)} %bitcast.31, pred[4,8]{1,0:T(4,128)(4,1)S(1)} %get-tuple-element.15, pred[4,8]{1,0:T(4,128)(4,1)S(1)} %get-tuple-element.16), kind=kOutput, calls=%fused_computation.3 | convolution fusion | flops 17825920 | bytes 3145792 | tf_op jit(solution)/shard_map/dqk,rky->dqry/dot_general | solution.py:455
  4.5 0.0 copy-start.1
  4.5 4.7 %all-to-all-start = ((bf16[4,4,512,128]{3,1,2,0:T(4,128)(2,1)}), bf16[4,4,512,128]{3,1,2,0:T(4,128)(2,1)S(1)}, u32[]{:S(2)}, u32[]{:S(2)}) async-start(bf16[4,4,512,128]{3,1,2,0:T(4,128)(2,1)} %convolution_convert_fusion), calls=%async_computation | async-start | bytes 4194304 | tf_op jit(solution)/shard_map/all_to_all | solution.py:468
  9.2 0.0 copy-done.1
  9.2 0.1 reshape.141
  9.3 0.1 constant_dynamic-slice_fusion
  9.4 0.1 copy.17
  9.5 0.1 copy.11
  9.6 0.1 copy.10
  9.7 44.7 %all-to-all-done = bf16[4,4,512,128]{3,1,2,0:T(4,128)(2,1)S(1)} async-done(((bf16[4,4,512,128]{3,1,2,0:T(4,128)(2,1)}), bf16[4,4,512,128]{3,1,2,0:T(4,128)(2,1)S(1)}, u32[]{:S(2)}, u32[]{:S(2)}) %all-to-all-start) | async-done | bytes 2097184 | tf_op jit(solution)/shard_map/all_to_all | solution.py:468
  54.5 3.7 %fusion.2 = f32[8,128,4,128]{3,0,1,2:T(8,128)S(1)} fusion(bf16[4,4,4,128,128]{4,1,3,2,0:T(4,128)(2,1)S(1)} %bitcast.32, s32[4,4]{0,1:T(4,128)S(1)} %copy.11, pred[4,4]{0,1:T(4,128)(4,1)S(1)} %copy.10), kind=kOutput, calls=%fused_computation.4 | convolution fusion | flops 16777472 | bytes 4194384 | tf_op jit(solution)/shard_map/ska,sqkyx->ayqx/dot_general | solution.py:471
  58.2 0.0 copy-start
  58.2 1.4 copy.13
  59.5 0.0 copy-done
  59.5 2.1 %fusion.22 = (bf16[1024,512]{1,0:T(8,128)(2,1)}, f32[1024,512]{1,0:T(8,128)}) fusion(f32[128,8,4,128]{3,2,1,0:T(4,128)S(1)} %bitcast.30, bf16[1024,512]{1,0:T(8,128)(2,1)S(1)} %copy-done), kind=kLoop, calls=%fused_computation.49 | loop fusion | flops 1572864 | bytes 6291456 | tf_op jit(solution)/shard_map/convert_element_type | solution.py:475
  61.7 70.4 %spread_panels.1 = (bf16[1024,512]{1,0:T(8,128)(2,1)}, bf16[512,512]{1,0:T(8,128)(2,1)}, bf16[512,512]{1,0:T(8,128)(2,1)}) custom-call(bf16[1024,512]{1,0:T(8,128)(2,1)} %get-tuple-element.11.front), custom_call_target="tpu_custom_call" | custom-call | tf_op jit(solution)/shard_map/spread_panels/pallas_call | solution.py:230
  132.1 40.9 %factor_and_update.1 = f32[1024,512]{1,0:T(8,128)} custom-call(bf16[512,512]{1,0:T(8,128)(2,1)} %get-tuple-element.8.lead, bf16[512,512]{1,0:T(8,128)(2,1)} %get-tuple-element.9.top, bf16[1024,512]{1,0:T(8,128)(2,1)} %get-tuple-element.10.panel, f32[1024,512]{1,0:T(8,128)} %get-tuple-element.12.front), custom_call_target="tpu_custom_call" | custom-call | tf_op jit(solution)/shard_map/factor_and_update/pallas_call | solution.py:414
  (5 shorter events, 0.1 us)
Async XLA Ops:
  4.5 4.7 %copy-start.1 = (s32[4,64]{1,0:T(4,128)S(1)}, s32[4,64]{1,0:T(4,128)}, u32[]{:S(2)}) copy-start(s32[4,64]{1,0:T(4,128)} %param.5) | copy-start | bytes 3076
  4.5 49.9 %all-to-all-start = ((bf16[4,4,512,128]{3,1,2,0:T(4,128)(2,1)}), bf16[4,4,512,128]{3,1,2,0:T(4,128)(2,1)S(1)}, u32[]{:S(2)}, u32[]{:S(2)}) async-start(bf16[4,4,512,128]{3,1,2,0:T(4,128)(2,1)} %convolution_convert_fusion), calls=%async_computation | async-start | bytes 4194304 | tf_op jit(solution)/shard_map/all_to_all | solution.py:468
  58.2 1.4 copy-start

commit v2 on v1

--- a/solution.py
+++ b/solution.py
@@ -44,7 +44,13 @@
     front,
     panel,
     top,
+    inv_high,
+    inv_low,
+    lower,
     lead,
+    work,
+    inverse,
+    block_inv,
     local_sem,
     top_send,
     top_cross,
@@ -136,25 +142,22 @@
         own_top.start()
         each(GROUP, 0, lambda j: top_scatter(j).start())
 
+    @pl.when(r == 0)
+    def _():
+        own_top.wait()
+
+    @pl.when(r != 0)
+    def _():
+        arrived(top_piece(i), top_recv.at[i])
+
     @pl.when(p == 0)
     def _():
+        each(n_sub, 0, lambda k: lead_down(k).start())
+        each(n_col, 0, lambda k: lead_along(k).start())
         own_panel.start()
         each(plane, 0, lambda q: panel_scatter(q).start())
         each(plane, 0, lambda q: panel_zero(q).start())
 
-    @pl.when(r == 0)
-    def _():
-        own_top.wait()
-
-    @pl.when(r != 0)
-    def _():
-        arrived(top_piece(i), top_recv.at[i])
-
-    @pl.when(p == 0)
-    def _():
-        each(n_sub, 0, lambda k: lead_down(k).start())
-        each(n_col, 0, lambda k: lead_along(k).start())
-
     @pl.when(half == 0)
     def _():
         top_over.start()
@@ -183,10 +186,16 @@
     @pl.when(p == 0)
     def _():
         own_lead.start()
+        own_lead.wait()
 
     @pl.when(p != 0)
     def _():
         each(GROUP, i, lambda j: arrived(lead_piece(j), lead_recv.at[j]))
+
+    factor_leading(lead, work, inverse, lower, block_inv, inv_high, inv_low)
+
+    @pl.when(p != 0)
+    def _():
         each(plane, p, lambda q: arrived(panel_piece(q), panel_recv.at[q]))
 
     @pl.when(r == 0)
@@ -205,7 +214,6 @@
     @pl.when(p == 0)
     def _():
         own_panel.wait()
-        own_lead.wait()
         each(plane, 0, lambda q: panel_scatter(q).wait_send())
         each(plane, 0, lambda q: panel_zero(q).wait_send())
         each(n_sub, 0, lambda k: lead_down(k).wait_send())
@@ -232,11 +240,17 @@
         out_shape=(
             jax.ShapeDtypeStruct((rows, width), jnp.bfloat16),
             jax.ShapeDtypeStruct((WIDTH, width), jnp.bfloat16),
-            jax.ShapeDtypeStruct((WIDTH, width), jnp.bfloat16),
+            jax.ShapeDtypeStruct((WIDTH, WIDTH), jnp.bfloat16),
+            jax.ShapeDtypeStruct((WIDTH, WIDTH), jnp.bfloat16),
+            jax.ShapeDtypeStruct((WIDTH, WIDTH), jnp.float32),
         ),
         in_specs=[vmem],
-        out_specs=(vmem, vmem, vmem),
+        out_specs=(vmem,) * 5,
         scratch_shapes=[
+            pltpu.VMEM((WIDTH, WIDTH), jnp.bfloat16),
+            pltpu.VMEM((WIDTH, WIDTH), jnp.float32),
+            pltpu.VMEM((WIDTH, WIDTH), jnp.float32),
+            pltpu.VMEM((TILE, TILE), jnp.float32),
             dma((3,)),
             dma((GROUP,)),
             dma(()),
@@ -255,18 +269,18 @@
     )(front16)
 
 
-def invert_block(load_group, store_rows):
+def invert_block(block, store_rows):
     sub = 8
-    groups = TILE // sub
-    lane = lax.broadcasted_iota(jnp.int32, (sub, TILE), 1)
-    line = lax.broadcasted_iota(jnp.int32, (sub, TILE), 0)
-    a = [load_group(g) for g in range(groups)]
-    m = [jnp.where(lane == line + sub * g, 1.0, 0.0).astype(jnp.float32) for g in range(groups)]
     b = 4
+    line = lax.broadcasted_iota(jnp.int32, (TILE, TILE), 0)
+    lane = lax.broadcasted_iota(jnp.int32, (TILE, TILE), 1)
+    a = block
+    m = jnp.where(lane == line, 1.0, 0.0).astype(jnp.float32)
+    done = 0
     for j0 in range(0, TILE, b):
-        g0, i0 = divmod(j0, sub)
-        rows_a = [jnp.broadcast_to(a[g0][i0 + k : i0 + k + 1, :], (sub, TILE)) for k in range(b)]
-        rows_m = [jnp.broadcast_to(m[g0][i0 + k : i0 + k + 1, :], (sub, TILE)) for k in range(b)]
+        i0 = j0 - done
+        rows_a = [jnp.broadcast_to(a[i0 + k : i0 + k + 1, :], (sub, TILE)) for k in range(b)]
+        rows_m = [jnp.broadcast_to(m[i0 + k : i0 + k + 1, :], (sub, TILE)) for k in range(b)]
         piv = [
             [
                 jnp.broadcast_to(rows_a[l][:, j0 + k : j0 + k + 1], (sub, TILE))
@@ -310,17 +324,19 @@
         if j0 + b == TILE:
             break
         va, vm = solve_back(solve(rows_a)), solve_back(x)
-        first = (j0 + b) // sub
-        for g in range(first, groups):
-            for k in range(b):
-                col = jnp.broadcast_to(a[g][:, j0 + k : j0 + k + 1], (sub, TILE))
-                if g == g0:
-                    col = jnp.where(line >= i0 + b, col, 0.0)
-                if k == 0:
-                    da, dm = col * va[0], col * vm[0]
-                else:
-                    da, dm = da + col * va[k], dm + col * vm[k]
-            a[g], m[g] = a[g] - da, m[g] - dm
+        drop = (j0 + b) // sub * sub - done
+        if drop:
+            a, m, done = a[drop:], m[drop:], done + drop
+        height = TILE - done
+        da = dm = None
+        for k in range(b):
+            col = jnp.broadcast_to(a[:, j0 + k : j0 + k + 1], (height, TILE))
+            if done < j0 + b:
+                col = jnp.where(line[:height] >= j0 + b - done, col, 0.0)
+            ta = col * jnp.broadcast_to(va[k][0:1], (height, TILE))
+            tm = col * jnp.broadcast_to(vm[k][0:1], (height, TILE))
+            da, dm = (ta, tm) if k == 0 else (da + ta, dm + tm)
+        a, m = a - da, m - dm
 
 
 def split(x):
@@ -339,56 +355,52 @@
     return mul(xh, yh, transposed) + (mul(xh, yl, transposed) + mul(xl, yh, transposed))
 
 
-def factor_kernel(lead, top, panel, front, out, work, inverse, lower, block_inv, right):
-    row_id = lax.axis_index("row")
-    block_id = lax.axis_index("sub") * lax.axis_size("col") + lax.axis_index("col")
+def factor_leading(lead, work, inverse, lower, block_inv, inv_high, inv_low):
     width = WIDTH
     work[...] = lead[...].astype(jnp.float32)
     row_of = lax.broadcasted_iota(jnp.int32, (width, width), 0)
     col_of = lax.broadcasted_iota(jnp.int32, (width, width), 1)
     inverse[...] = jnp.where(row_of == col_of, 1.0, 0.0).astype(jnp.float32)
-    lower[...] = jnp.zeros_like(lower)
-
-    for kb in range(PANEL):
-        o = kb * TILE
-
-        def load_group(g):
-            return work[o + 8 * g : o + 8 * g + 8, o : o + TILE]
-
-        def store_rows(j0, x):
-            for k in range(len(x)):
-                block_inv[j0 + k : j0 + k + 1, :] = x[k][0:1, :]
-
-        invert_block(load_group, store_rows)
+
+    def store_rows(j0, x):
+        for k in range(len(x)):
+            block_inv[j0 + k : j0 + k + 1, :] = x[k][0:1, :]
+
+    def step(kb, _):
+        o = pl.multiple_of(kb * TILE, TILE)
+        here = pl.ds(o, TILE)
+        invert_block(work[here, here], store_rows)
         d_inv = block_inv[...]
-        rest = width - o - TILE
-        diag = mul3(work[o : o + TILE, o : o + TILE], d_inv, True)
-        tri = lax.broadcasted_iota(jnp.int32, (TILE, TILE), 0) >= lax.broadcasted_iota(
-            jnp.int32, (TILE, TILE), 1
-        )
-        lower[o : o + TILE, o : o + TILE] = jnp.where(tri, diag, 0.0)
-        x_rows = mul3(d_inv, inverse[o : o + TILE, 0 : o + TILE])
-        inverse[o : o + TILE, 0 : o + TILE] = x_rows
-        if rest:
-            below = mul3(work[o + TILE :, o : o + TILE], d_inv, True)
-            lower[o + TILE :, o : o + TILE] = below
-            work[o + TILE :, o + TILE :] = work[o + TILE :, o + TILE :] - mul3(below, below, True)
-            inverse[o + TILE :, 0 : o + TILE] = inverse[o + TILE :, 0 : o + TILE] - mul3(
-                below, x_rows
-            )
-
-    inv_high, inv_low = split(inverse[...])
+        below = mul3(work[:, here], d_inv, True)
+        line = lax.broadcasted_iota(jnp.int32, (width, TILE), 0)
+        lane = lax.broadcasted_iota(jnp.int32, (width, TILE), 1)
+        lower[:, here] = jnp.where(line >= lane + o, below, 0.0)
+        below = jnp.where(line >= o + TILE, below, 0.0)
+        x_rows = mul3(d_inv, inverse[here, :])
+        inverse[here, :] = x_rows
+        work[...] = work[...] - mul3(below, below, True)
+        inverse[...] = inverse[...] - mul3(below, x_rows)
+        return 0
+
+    lax.fori_loop(0, PANEL, step, 0)
+    high, low = split(inverse[...])
+    inv_high[...] = high
+    inv_low[...] = low
+
+
+def update_kernel(inv_high, inv_low, lower, top, panel, front, out, right):
+    row_id = lax.axis_index("row")
+    block_id = lax.axis_index("sub") * lax.axis_size("col") + lax.axis_index("col")
     tops = top[...]
-    right[...] = mul(inv_high, tops) + mul(inv_low, tops)
+    right[...] = mul(inv_high[...], tops) + mul(inv_low[...], tops)
     chunk = 128
 
     @pl.loop(0, panel.shape[0] // chunk)
     def _(t):
         rows = pl.ds(pl.multiple_of(t * chunk, chunk), chunk)
         a_rows = panel[rows, :]
-        xh, xl = split(inverse[...])
-        f_rows = mul(a_rows, xh, True) + mul(a_rows, xl, True)
-        head = (row_id == 0) & (t < width // chunk)
+        f_rows = mul(a_rows, inv_high[...], True) + mul(a_rows, inv_low[...], True)
+        head = (row_id == 0) & (t < WIDTH // chunk)
 
         @pl.when(block_id == 0)
         def _():
@@ -409,22 +421,16 @@
                 out[rows, :] = front[rows, :] - mul3(f_rows, right[...])
 
 
-def factor_and_update(lead, top, panel, front):
+def apply_update(inv_high, inv_low, lower, top, panel, front):
     vmem = pl.BlockSpec(memory_space=pltpu.VMEM)
     return pl.pallas_call(
-        factor_kernel,
+        update_kernel,
         out_shape=jax.ShapeDtypeStruct(front.shape, jnp.float32),
-        in_specs=[vmem] * 4,
+        in_specs=[vmem] * 6,
         out_specs=vmem,
-        scratch_shapes=[
-            pltpu.VMEM((WIDTH, WIDTH), jnp.float32),
-            pltpu.VMEM((WIDTH, WIDTH), jnp.float32),
-            pltpu.VMEM((WIDTH, WIDTH), jnp.float32),
-            pltpu.VMEM((TILE, TILE), jnp.float32),
-            pltpu.VMEM((WIDTH, WIDTH), jnp.float32),
-        ],
-        name="factor_and_update",
-    )(lead, top, panel, front)
+        scratch_shapes=[pltpu.VMEM((WIDTH, WIDTH), jnp.float32)],
+        name="apply_update",
+    )(inv_high, inv_low, lower, top, panel, front)
 
 
 def body(child_update, parent_front, tile_map):
@@ -471,10 +477,10 @@
     spread = jnp.einsum("ska,sqkyx->ayqx", place_row, grid, preferred_element_type=jnp.float32)
     placed = spread.reshape(front_rows * tile_len, slot_count * tile_len)
     front_local = parent_front.astype(jnp.float32) + placed
-    panel, top, lead = spread_panels(
+    panel, top, inv_high, inv_low, lower = spread_panels(
         front_local.astype(jnp.bfloat16), sub_count, row_count, col_count
     )
-    return factor_and_update(lead, top, panel, front_local)
+    return apply_update(inv_high, inv_low, lower, top, panel, front_local)
 
 
 def solution(mesh):

time: 173 us -> 181 us (1.046)
  the two profiles are of different devices: /device:TPU:481 before, /device:TPU:353 now
where the time goes in v2:
time: 181 us
  Pallas kernels  120 us (66%)
  waiting for transfers between devices  43.8 us (24%)
  matrix products  5.72 us (3%)
  starting transfers between devices  4.68 us (3%)
  local copies, waits for them, and re-layouts  4.29 us (2%)
  other arithmetic  2.19 us (1%)
    pallas_call x1, Pallas kernels, spread_panels(): pl.pallas_call(functools.partial(spread_kernel, n_sub, n_row, n_col), out...  108 us
    all_to_all x1, waiting for transfers between devices, body(): lax.all_to_all(payload, 'sub', split_axis=0, concat_axis=0, tiled=True)  43.8 us
    pallas_call x1, Pallas kernels, apply_update(): pl.pallas_call(update_kernel, out_shape=jax.ShapeDtypeStruct(front.shape,...  11.8 us
    all_to_all x1, starting transfers between devices, body(): lax.all_to_all(payload, 'sub', split_axis=0, concat_axis=0, tiled=True)  4.68 us
    dot_general x1, matrix products, body(): jnp.einsum('ska,sqkyx->ayqx', place_row, grid, preferred_element_type=jnp...  3.68 us
  transfers between devices with their start and end apart: 1, of which 1 were waited for; matrix products, arithmetic and copies ran while one was open for 0% of the time, Pallas kernels for 0%

profile of v2, /device:TPU:353, one launch (start us, length us, event | category | flops | bytes accessed | tf_op | source)
XLA Modules:
  0.0 180.6 jit_solution(15367400143698880659)
XLA Ops:
  0.0 0.7 fusion.21
  0.7 0.1 reshape.138
  0.8 0.2 dynamic-slice_reduce_fusion
  1.0 1.5 copy.18
  2.5 2.0 %convolution_convert_fusion = bf16[4,4,512,128]{3,1,2,0:T(4,128)(2,1)} fusion(bf16[512,8,128,1]{2,1,0,3:T(8,128)(2,1)S(1)} %bitcast.31, pred[4,8]{1,0:T(4,128)(4,1)S(1)} %get-tuple-element.19, pred[4,8]{1,0:T(4,128)(4,1)S(1)} %get-tuple-element.20), kind=kOutput, calls=%fused_computation.3 | convolution fusion | flops 17825920 | bytes 3145792 | tf_op jit(solution)/shard_map/dqk,rky->dqry/dot_general | solution.py:461
  4.5 0.0 copy-start.1
  4.6 4.7 %all-to-all-start = ((bf16[4,4,512,128]{3,1,2,0:T(4,128)(2,1)}), bf16[4,4,512,128]{3,1,2,0:T(4,128)(2,1)S(1)}, u32[]{:S(2)}, u32[]{:S(2)}) async-start(bf16[4,4,512,128]{3,1,2,0:T(4,128)(2,1)} %convolution_convert_fusion), calls=%async_computation | async-start | bytes 4194304 | tf_op jit(solution)/shard_map/all_to_all | solution.py:474
  9.2 0.0 copy-done.1
  9.2 0.1 reshape.141
  9.3 0.1 constant_dynamic-slice_fusion
  9.4 0.1 copy.17
  9.5 0.1 copy.11
  9.6 0.1 copy.10
  9.7 43.8 %all-to-all-done = bf16[4,4,512,128]{3,1,2,0:T(4,128)(2,1)S(1)} async-done(((bf16[4,4,512,128]{3,1,2,0:T(4,128)(2,1)}), bf16[4,4,512,128]{3,1,2,0:T(4,128)(2,1)S(1)}, u32[]{:S(2)}, u32[]{:S(2)}) %all-to-all-start) | async-done | bytes 2097184 | tf_op jit(solution)/shard_map/all_to_all | solution.py:474
  53.6 3.7 %fusion.2 = f32[8,128,4,128]{3,0,1,2:T(8,128)S(1)} fusion(bf16[4,4,4,128,128]{4,1,3,2,0:T(4,128)(2,1)S(1)} %bitcast.32, s32[4,4]{0,1:T(4,128)S(1)} %copy.11, pred[4,4]{0,1:T(4,128)(4,1)S(1)} %copy.10), kind=kOutput, calls=%fused_computation.4 | convolution fusion | flops 16777472 | bytes 4194384 | tf_op jit(solution)/shard_map/ska,sqkyx->ayqx/dot_general | solution.py:477
  57.3 0.0 copy-start
  57.3 1.4 copy.13
  58.6 0.0 copy-done
  58.6 2.1 %fusion.22 = (bf16[1024,512]{1,0:T(8,128)(2,1)}, f32[1024,512]{1,0:T(8,128)}) fusion(f32[128,8,4,128]{3,2,1,0:T(4,128)S(1)} %bitcast.30, bf16[1024,512]{1,0:T(8,128)(2,1)S(1)} %copy-done), kind=kLoop, calls=%fused_computation.49 | loop fusion | flops 1572864 | bytes 6291456 | tf_op jit(solution)/shard_map/convert_element_type | solution.py:481
  60.8 108.0 %spread_panels.1 = (bf16[1024,512]{1,0:T(8,128)(2,1)}, bf16[512,512]{1,0:T(8,128)(2,1)}, bf16[512,512]{1,0:T(8,128)(2,1)}, bf16[512,512]{1,0:T(8,128)(2,1)}, f32[512,512]{1,0:T(8,128)}) custom-call(bf16[1024,512]{1,0:T(8,128)(2,1)} %get-tuple-element.15.front), custom_call_target="tpu_custom_call" | custom-call | tf_op jit(solution)/shard_map/spread_panels/pallas_call | solution.py:238
  168.7 11.8 %apply_update.1 = f32[1024,512]{1,0:T(8,128)} custom-call(bf16[512,512]{1,0:T(8,128)(2,1)} %get-tuple-element.10.inv_high, bf16[512,512]{1,0:T(8,128)(2,1)} %get-tuple-element.11.inv_low, f32[512,512]{1,0:T(8,128)} %get-tuple-element.12.lower, bf16[512,512]{1,0:T(8,128)(2,1)} %get-tuple-element.13.top, bf16[1024,512]{1,0:T(8,128)(2,1)} %get-tuple-element.14.panel, ...), custom_call_target="tpu_custom_call" | custom-call | tf_op jit(solution)/shard_map/apply_update/pallas_call | solution.py:426
  (5 shorter events, 0.1 us)
Async XLA Ops:
  4.5 4.7 %copy-start.1 = (s32[4,64]{1,0:T(4,128)S(1)}, s32[4,64]{1,0:T(4,128)}, u32[]{:S(2)}) copy-start(s32[4,64]{1,0:T(4,128)} %param.5) | copy-start | bytes 3076
  4.6 49.0 %all-to-all-start = ((bf16[4,4,512,128]{3,1,2,0:T(4,128)(2,1)}), bf16[4,4,512,128]{3,1,2,0:T(4,128)(2,1)S(1)}, u32[]{:S(2)}, u32[]{:S(2)}) async-start(bf16[4,4,512,128]{3,1,2,0:T(4,128)(2,1)} %convolution_convert_fusion), calls=%async_computation | async-start | bytes 4194304 | tf_op jit(solution)/shard_map/all_to_all | solution.py:474
  57.3 1.4 copy-start

commit v3 on v2

--- a/solution.py
+++ b/solution.py
@@ -137,47 +137,53 @@
     def arrived(piece, sem):
         pltpu.make_async_copy(piece, piece, sem).wait()
 
+    def share_top():
+        each(GROUP, i, lambda j: pl.when((j != 0) | (half != 0))(lambda: top_share(j).start()))
+
     @pl.when(r == 0)
     def _():
         own_top.start()
         each(GROUP, 0, lambda j: top_scatter(j).start())
-
-    @pl.when(r == 0)
-    def _():
         own_top.wait()
 
-    @pl.when(r != 0)
+    @pl.when((r != 0) & (half == 0))
     def _():
         arrived(top_piece(i), top_recv.at[i])
 
+    @pl.when(half == 0)
+    def _():
+        top_over.start()
+
     @pl.when(p == 0)
     def _():
+        @pl.when(half != 0)
+        def _():
+            arrived(top_piece(i), top_recv.at[i])
+
         each(n_sub, 0, lambda k: lead_down(k).start())
         each(n_col, 0, lambda k: lead_along(k).start())
         own_panel.start()
         each(plane, 0, lambda q: panel_scatter(q).start())
+        share_top()
         each(plane, 0, lambda q: panel_zero(q).start())
 
-    @pl.when(half == 0)
-    def _():
-        top_over.start()
-        each(GROUP, i, lambda j: pl.when(j != 0)(lambda: top_share(j).start()))
-
-    @pl.when(half != 0)
-    def _():
-        each(GROUP, i, lambda j: top_share(j).start())
-
     @pl.when(p != 0)
     def _():
+        arrived(lead_piece(i), lead_recv.at[i])
+
+        @pl.when(c == 0)
+        def _():
+            each(n_col, 0, lambda k: lead_forward(k).start())
+
+        each(GROUP, i, lambda j: lead_share(j).start())
+
+        @pl.when(half != 0)
+        def _():
+            arrived(top_piece(i), top_recv.at[i])
+
+        share_top()
         arrived(panel_piece(p), panel_recv.at[p])
         each(plane, p, lambda q: pl.when(q != 0)(lambda: panel_share(q).start()))
-        arrived(lead_piece(i), lead_recv.at[i])
-
-        @pl.when(c == 0)
-        def _():
-            each(n_col, 0, lambda k: lead_forward(k).start())
-
-        each(GROUP, i, lambda j: lead_share(j).start())
 
     @pl.when(r != 0)
     def _():

time: 181 us -> 168 us (0.928)
  the two profiles are of different devices: /device:TPU:353 before, /device:TPU:486 now
where the time goes in v3:
time: 168 us; the launch traced here: 167 us
  Pallas kernels  105 us (62%)
  waiting for transfers between devices  45.3 us (27%)
  matrix products  5.72 us (3%)
  starting transfers between devices  5.22 us (3%)
  local copies, waits for them, and re-layouts  4.29 us (3%)
  other arithmetic  2.19 us (1%)
    pallas_call x1, Pallas kernels, spread_panels(): pl.pallas_call(functools.partial(spread_kernel, n_sub, n_row, n_col), out...  92.8 us
    all_to_all x1, waiting for transfers between devices, body(): lax.all_to_all(payload, 'sub', split_axis=0, concat_axis=0, tiled=True)  45.3 us
    pallas_call x1, Pallas kernels, apply_update(): pl.pallas_call(update_kernel, out_shape=jax.ShapeDtypeStruct(front.shape,...  11.8 us
    all_to_all x1, starting transfers between devices, body(): lax.all_to_all(payload, 'sub', split_axis=0, concat_axis=0, tiled=True)  5.22 us
    dot_general x1, matrix products, body(): jnp.einsum('ska,sqkyx->ayqx', place_row, grid, preferred_element_type=jnp...  3.69 us
  transfers between devices with their start and end apart: 1, of which 1 were waited for; matrix products, arithmetic and copies ran while one was open for 0% of the time, Pallas kernels for 0%

profile of v3, /device:TPU:486, one launch (start us, length us, event | category | flops | bytes accessed | tf_op | source)
XLA Modules:
  0.0 167.4 jit_solution(264955769004027447)
XLA Ops:
  0.0 0.7 fusion.21
  0.7 0.1 reshape.138
  0.8 0.2 dynamic-slice_reduce_fusion
  1.0 1.5 copy.18
  2.5 2.0 %convolution_convert_fusion = bf16[4,4,512,128]{3,1,2,0:T(4,128)(2,1)} fusion(bf16[512,8,128,1]{2,1,0,3:T(8,128)(2,1)S(1)} %bitcast.31, pred[4,8]{1,0:T(4,128)(4,1)S(1)} %get-tuple-element.19, pred[4,8]{1,0:T(4,128)(4,1)S(1)} %get-tuple-element.20), kind=kOutput, calls=%fused_computation.3 | convolution fusion | flops 17825920 | bytes 3145792 | tf_op jit(solution)/shard_map/dqk,rky->dqry/dot_general | solution.py:467
  4.5 0.0 copy-start.1
  4.5 5.2 %all-to-all-start = ((bf16[4,4,512,128]{3,1,2,0:T(4,128)(2,1)}), bf16[4,4,512,128]{3,1,2,0:T(4,128)(2,1)S(1)}, u32[]{:S(2)}, u32[]{:S(2)}) async-start(bf16[4,4,512,128]{3,1,2,0:T(4,128)(2,1)} %convolution_convert_fusion), calls=%async_computation | async-start | bytes 4194304 | tf_op jit(solution)/shard_map/all_to_all | solution.py:480
  9.8 0.0 copy-done.1
  9.8 0.1 reshape.141
  9.9 0.1 constant_dynamic-slice_fusion
  9.9 0.1 copy.17
  10.1 0.1 copy.11
  10.2 0.1 copy.10
  10.3 45.3 %all-to-all-done = bf16[4,4,512,128]{3,1,2,0:T(4,128)(2,1)S(1)} async-done(((bf16[4,4,512,128]{3,1,2,0:T(4,128)(2,1)}), bf16[4,4,512,128]{3,1,2,0:T(4,128)(2,1)S(1)}, u32[]{:S(2)}, u32[]{:S(2)}) %all-to-all-start) | async-done | bytes 2097184 | tf_op jit(solution)/shard_map/all_to_all | solution.py:480
  55.6 3.7 %fusion.2 = f32[8,128,4,128]{3,0,1,2:T(8,128)S(1)} fusion(bf16[4,4,4,128,128]{4,1,3,2,0:T(4,128)(2,1)S(1)} %bitcast.32, s32[4,4]{0,1:T(4,128)S(1)} %copy.11, pred[4,4]{0,1:T(4,128)(4,1)S(1)} %copy.10), kind=kOutput, calls=%fused_computation.4 | convolution fusion | flops 16777472 | bytes 4194384 | tf_op jit(solution)/shard_map/ska,sqkyx->ayqx/dot_general | solution.py:483
  59.3 0.0 copy-start
  59.3 1.4 copy.13
  60.7 0.0 copy-done
  60.7 2.1 %fusion.22 = (bf16[1024,512]{1,0:T(8,128)(2,1)}, f32[1024,512]{1,0:T(8,128)}) fusion(f32[128,8,4,128]{3,2,1,0:T(4,128)S(1)} %bitcast.30, bf16[1024,512]{1,0:T(8,128)(2,1)S(1)} %copy-done), kind=kLoop, calls=%fused_computation.49 | loop fusion | flops 1572864 | bytes 6291456 | tf_op jit(solution)/shard_map/convert_element_type | solution.py:487
  62.8 92.8 %spread_panels.1 = (bf16[1024,512]{1,0:T(8,128)(2,1)}, bf16[512,512]{1,0:T(8,128)(2,1)}, bf16[512,512]{1,0:T(8,128)(2,1)}, bf16[512,512]{1,0:T(8,128)(2,1)}, f32[512,512]{1,0:T(8,128)}) custom-call(bf16[1024,512]{1,0:T(8,128)(2,1)} %get-tuple-element.15.front), custom_call_target="tpu_custom_call" | custom-call | tf_op jit(solution)/shard_map/spread_panels/pallas_call | solution.py:244
  155.6 11.8 %apply_update.1 = f32[1024,512]{1,0:T(8,128)} custom-call(bf16[512,512]{1,0:T(8,128)(2,1)} %get-tuple-element.10.inv_high, bf16[512,512]{1,0:T(8,128)(2,1)} %get-tuple-element.11.inv_low, f32[512,512]{1,0:T(8,128)} %get-tuple-element.12.lower, bf16[512,512]{1,0:T(8,128)(2,1)} %get-tuple-element.13.top, bf16[1024,512]{1,0:T(8,128)(2,1)} %get-tuple-element.14.panel, ...), custom_call_target="tpu_custom_call" | custom-call | tf_op jit(solution)/shard_map/apply_update/pallas_call | solution.py:432
  (5 shorter events, 0.1 us)
Async XLA Ops:
  4.5 5.2 %copy-start.1 = (s32[4,64]{1,0:T(4,128)S(1)}, s32[4,64]{1,0:T(4,128)}, u32[]{:S(2)}) copy-start(s32[4,64]{1,0:T(4,128)} %param.5) | copy-start | bytes 3076
  4.5 51.1 %all-to-all-start = ((bf16[4,4,512,128]{3,1,2,0:T(4,128)(2,1)}), bf16[4,4,512,128]{3,1,2,0:T(4,128)(2,1)S(1)}, u32[]{:S(2)}, u32[]{:S(2)}) async-start(bf16[4,4,512,128]{3,1,2,0:T(4,128)(2,1)} %convolution_convert_fusion), calls=%async_computation | async-start | bytes 4194304 | tf_op jit(solution)/shard_map/all_to_all | solution.py:480
  59.3 1.4 copy-start

commit v4 on v3

--- a/solution.py
+++ b/solution.py
@@ -56,22 +56,21 @@
     top_cross,
     top_gather,
     top_recv,
-    panel_send,
-    panel_first,
+    panel_col,
+    panel_sub,
     panel_recv,
+    panel_far,
+    ring_right,
+    ring_left,
     lead_sub,
     lead_col,
     lead_gather,
     lead_recv,
 ):
     s, r, c = lax.axis_index("sub"), lax.axis_index("row"), lax.axis_index("col")
-    plane = n_sub * n_col
     p = s * n_col + c
     half, i = r // GROUP, r % GROUP
-    depth = front.shape[0] // plane
-
-    def at_plane(q):
-        return (q // n_col, r, q % n_col)
+    depth = front.shape[0] // n_col
 
     def at_group(j):
         return (s, half * GROUP + j, c)
@@ -97,27 +96,64 @@
     def greet(device):
         pl.semaphore_signal(barrier, inc=1, device_id=device, device_id_type=MESH)
 
-    each(plane, p, lambda q: greet(at_plane(q)))
+    each(n_sub, s, lambda k: greet((k, r, c)))
+    each(n_col, c, lambda k: greet((s, r, k)))
     each(GROUP, i, lambda j: greet(at_group(j)))
     greet(across)
-    pl.semaphore_wait(barrier, plane - 1 + GROUP - 1 + 1)
+    pl.semaphore_wait(barrier, n_sub - 1 + n_col - 1 + GROUP - 1 + 1)
 
     top_scatter = lambda j: remote(
         front_top(j), top_piece(j), top_send.at[j], top_recv.at[j], at_group(j)
     )
-    panel_scatter = lambda q: remote(
-        front_piece(q), panel_piece(q), panel_send.at[q], panel_recv.at[q], at_plane(q)
-    )
-    panel_zero = lambda q: remote(
-        front_piece(0), panel_piece(0), panel_first.at[q], panel_recv.at[0], at_plane(q)
-    )
+    panel_along = lambda k: remote(
+        front_piece(k), panel_piece(k), panel_col.at[k], panel_recv.at[k], (0, r, k)
+    )
+    root_down = lambda k: remote(
+        front_piece(0), panel_piece(0), panel_sub.at[k], panel_recv.at[0], (k, r, 0)
+    )
+    panel_down = lambda k: remote(
+        panel_piece(c), panel_piece(c), panel_sub.at[k], panel_recv.at[c], (k, r, c)
+    )
+    right, left = (c + 1) % n_col, (c + n_col - 1) % n_col
+    last = n_col // 2
+
+    def from_left(t):
+        return (c + n_col - t) % n_col
+
+    def from_right(t):
+        return (c + t) % n_col
+
+    def ring_copies(t):
+        go_right, go_left = panel_piece(from_left(t - 1)), panel_piece(from_right(t - 1))
+        left_sem = panel_recv.at[from_right(t - 1)]
+        if t == last:
+            go_right = go_right.at[pl.ds(0, depth // 2)]
+            go_left = go_left.at[pl.ds(depth // 2, depth // 2)]
+            left_sem = panel_far
+        return (
+            remote(
+                go_right, go_right, ring_right.at[t], panel_recv.at[from_left(t - 1)], (s, r, right)
+            ),
+            remote(go_left, go_left, ring_left.at[t], left_sem, (s, r, left)),
+        )
+
+    to_right, to_left = (s != 0) | (right != 0), (s != 0) | (left != 0)
+
+    def ring_step(t):
+        @pl.when((p != 0) & ((t > 1) | (s != 0)))
+        def _():
+            arrived(panel_piece(from_left(t - 1)), panel_recv.at[from_left(t - 1)])
+            if t > 1:
+                arrived(panel_piece(from_right(t - 1)), panel_recv.at[from_right(t - 1)])
+
+        go_right, go_left = ring_copies(t)
+        pl.when(to_right)(go_right.start)
+        pl.when(to_left)(go_left.start)
+
     top_over = remote(top_piece(i), top_piece(i), top_cross, top_recv.at[i], across)
     top_share = lambda j: remote(
         top_piece(i), top_piece(i), top_gather.at[j], top_recv.at[i], at_group(j)
     )
-    panel_share = lambda q: remote(
-        panel_piece(p), panel_piece(p), panel_send.at[q], panel_recv.at[p], at_plane(q)
-    )
     lead_down = lambda k: remote(
         top_piece(i), lead_piece(i), lead_sub.at[k], lead_recv.at[i], (k, r, 0)
     )
@@ -163,9 +199,11 @@
         each(n_sub, 0, lambda k: lead_down(k).start())
         each(n_col, 0, lambda k: lead_along(k).start())
         own_panel.start()
-        each(plane, 0, lambda q: panel_scatter(q).start())
+        each(n_sub, 0, lambda k: root_down(k).start())
+        for k in sorted(range(1, n_col), key=lambda k: -min(k, n_col - k)):
+            panel_along(k).start()
         share_top()
-        each(plane, 0, lambda q: panel_zero(q).start())
+        own_panel.wait()
 
     @pl.when(p != 0)
     def _():
@@ -182,12 +220,16 @@
             arrived(top_piece(i), top_recv.at[i])
 
         share_top()
-        arrived(panel_piece(p), panel_recv.at[p])
-        each(plane, p, lambda q: pl.when(q != 0)(lambda: panel_share(q).start()))
-
-    @pl.when(r != 0)
-    def _():
+
+        @pl.when(s == 0)
+        def _():
+            arrived(panel_piece(c), panel_recv.at[c])
+            each(n_sub, 0, lambda k: panel_down(k).start())
+
+    def all_of_top():
         each(GROUP, i, lambda j: arrived(top_piece(j), top_recv.at[j]))
+
+    pl.when((r != 0) & (p == 0))(all_of_top)
 
     @pl.when(p == 0)
     def _():
@@ -198,11 +240,21 @@
     def _():
         each(GROUP, i, lambda j: arrived(lead_piece(j), lead_recv.at[j]))
 
-    factor_leading(lead, work, inverse, lower, block_inv, inv_high, inv_low)
+    def between(kb):
+        for t in range(1, last):
+            pl.when(kb == t)(functools.partial(ring_step, t))
+
+    factor_leading(lead, work, inverse, lower, block_inv, inv_high, inv_low, between)
+    ring_step(last)
+
+    pl.when((r != 0) & (p != 0))(all_of_top)
 
     @pl.when(p != 0)
     def _():
-        each(plane, p, lambda q: arrived(panel_piece(q), panel_recv.at[q]))
+        low = panel_piece(from_left(last)).at[pl.ds(0, depth // 2)]
+        high = panel_piece(from_left(last)).at[pl.ds(depth // 2, depth // 2)]
+        arrived(low, panel_recv.at[from_left(last)])
+        arrived(high, panel_far)
 
     @pl.when(r == 0)
     def _():
@@ -219,28 +271,33 @@
 
     @pl.when(p == 0)
     def _():
-        own_panel.wait()
-        each(plane, 0, lambda q: panel_scatter(q).wait_send())
-        each(plane, 0, lambda q: panel_zero(q).wait_send())
+        each(n_sub, 0, lambda k: root_down(k).wait_send())
+        each(n_col, 0, lambda k: panel_along(k).wait_send())
         each(n_sub, 0, lambda k: lead_down(k).wait_send())
         each(n_col, 0, lambda k: lead_along(k).wait_send())
 
     @pl.when(p != 0)
     def _():
-        each(plane, p, lambda q: pl.when(q != 0)(lambda: panel_share(q).wait_send()))
+        @pl.when(s == 0)
+        def _():
+            each(n_sub, 0, lambda k: panel_down(k).wait_send())
 
         @pl.when(c == 0)
         def _():
             each(n_col, 0, lambda k: lead_forward(k).wait_send())
 
         each(GROUP, i, lambda j: lead_share(j).wait_send())
+
+    for t in range(1, last + 1):
+        go_right, go_left = ring_copies(t)
+        pl.when(to_right)(go_right.wait_send)
+        pl.when(to_left)(go_left.wait_send)
 
 
 def spread_panels(front16, n_sub, n_row, n_col):
     rows, width = front16.shape
     vmem = pl.BlockSpec(memory_space=pltpu.VMEM)
     dma = pltpu.SemaphoreType.DMA
-    plane = n_sub * n_col
     return pl.pallas_call(
         functools.partial(spread_kernel, n_sub, n_row, n_col),
         out_shape=(
@@ -262,9 +319,12 @@
             dma(()),
             dma((GROUP,)),
             dma((GROUP,)),
-            dma((plane,)),
-            dma((plane,)),
-            dma((plane,)),
+            dma((n_col,)),
+            dma((n_sub,)),
+            dma((n_col,)),
+            dma(()),
+            dma((n_col,)),
+            dma((n_col,)),
             dma((n_sub,)),
             dma((n_col,)),
             dma((GROUP,)),
@@ -361,7 +421,7 @@
     return mul(xh, yh, transposed) + (mul(xh, yl, transposed) + mul(xl, yh, transposed))
 
 
-def factor_leading(lead, work, inverse, lower, block_inv, inv_high, inv_low):
+def factor_leading(lead, work, inverse, lower, block_inv, inv_high, inv_low, between):
     width = WIDTH
     work[...] = lead[...].astype(jnp.float32)
     row_of = lax.broadcasted_iota(jnp.int32, (width, width), 0)
@@ -373,6 +433,7 @@
             block_inv[j0 + k : j0 + k + 1, :] = x[k][0:1, :]
 
     def step(kb, _):
+        between(kb)
         o = pl.multiple_of(kb * TILE, TILE)
         here = pl.ds(o, TILE)
         invert_block(work[here, here], store_rows)

time: 168 us -> 153 us (0.911)
  the two profiles are of different devices: /device:TPU:486 before, /device:TPU:449 now
where the time goes in v4:
time: 153 us; the launch traced here: 151 us
  Pallas kernels  89.3 us (58%)
  waiting for transfers between devices  44.7 us (29%)
  matrix products  5.72 us (4%)
  starting transfers between devices  4.66 us (3%)
  local copies, waits for them, and re-layouts  4.29 us (3%)
  other arithmetic  2.19 us (1%)
    pallas_call x1, Pallas kernels, spread_panels(): pl.pallas_call(functools.partial(spread_kernel, n_sub, n_row, n_col), out...  77.5 us
    all_to_all x1, waiting for transfers between devices, body(): lax.all_to_all(payload, 'sub', split_axis=0, concat_axis=0, tiled=True)  44.7 us
    pallas_call x1, Pallas kernels, apply_update(): pl.pallas_call(update_kernel, out_shape=jax.ShapeDtypeStruct(front.shape,...  11.9 us
    all_to_all x1, starting transfers between devices, body(): lax.all_to_all(payload, 'sub', split_axis=0, concat_axis=0, tiled=True)  4.66 us
    dot_general x1, matrix products, body(): jnp.einsum('ska,sqkyx->ayqx', place_row, grid, preferred_element_type=jnp...  3.69 us
  transfers between devices with their start and end apart: 1, of which 1 were waited for; matrix products, arithmetic and copies ran while one was open for 0% of the time, Pallas kernels for 0%

profile of v4, /device:TPU:449, one launch (start us, length us, event | category | flops | bytes accessed | tf_op | source)
XLA Modules:
  0.0 151.0 jit_solution(12548676401429082711)
XLA Ops:
  0.0 0.7 fusion.21
  0.7 0.1 reshape.138
  0.8 0.2 dynamic-slice_reduce_fusion
  1.0 1.5 copy.18
  2.5 2.0 %convolution_convert_fusion = bf16[4,4,512,128]{3,1,2,0:T(4,128)(2,1)} fusion(bf16[512,8,128,1]{2,1,0,3:T(8,128)(2,1)S(1)} %bitcast.31, pred[4,8]{1,0:T(4,128)(4,1)S(1)} %get-tuple-element.19, pred[4,8]{1,0:T(4,128)(4,1)S(1)} %get-tuple-element.20), kind=kOutput, calls=%fused_computation.3 | convolution fusion | flops 17825920 | bytes 3145792 | tf_op jit(solution)/shard_map/dqk,rky->dqry/dot_general | solution.py:528
  4.5 0.0 copy-start.1
  4.6 4.7 %all-to-all-start = ((bf16[4,4,512,128]{3,1,2,0:T(4,128)(2,1)}), bf16[4,4,512,128]{3,1,2,0:T(4,128)(2,1)S(1)}, u32[]{:S(2)}, u32[]{:S(2)}) async-start(bf16[4,4,512,128]{3,1,2,0:T(4,128)(2,1)} %convolution_convert_fusion), calls=%async_computation | async-start | bytes 4194304 | tf_op jit(solution)/shard_map/all_to_all | solution.py:541
  9.2 0.0 copy-done.1
  9.2 0.1 reshape.141
  9.3 0.1 constant_dynamic-slice_fusion
  9.4 0.1 copy.17
  9.5 0.1 copy.11
  9.6 0.1 copy.10
  9.7 44.7 %all-to-all-done = bf16[4,4,512,128]{3,1,2,0:T(4,128)(2,1)S(1)} async-done(((bf16[4,4,512,128]{3,1,2,0:T(4,128)(2,1)}), bf16[4,4,512,128]{3,1,2,0:T(4,128)(2,1)S(1)}, u32[]{:S(2)}, u32[]{:S(2)}) %all-to-all-start) | async-done | bytes 2097184 | tf_op jit(solution)/shard_map/all_to_all | solution.py:541
  54.5 3.7 %fusion.2 = f32[8,128,4,128]{3,0,1,2:T(8,128)S(1)} fusion(bf16[4,4,4,128,128]{4,1,3,2,0:T(4,128)(2,1)S(1)} %bitcast.32, s32[4,4]{0,1:T(4,128)S(1)} %copy.11, pred[4,4]{0,1:T(4,128)(4,1)S(1)} %copy.10), kind=kOutput, calls=%fused_computation.4 | convolution fusion | flops 16777472 | bytes 4194384 | tf_op jit(solution)/shard_map/ska,sqkyx->ayqx/dot_general | solution.py:544
  58.2 0.0 copy-start
  58.2 1.4 copy.13
  59.5 0.0 copy-done
  59.5 2.1 %fusion.22 = (bf16[1024,512]{1,0:T(8,128)(2,1)}, f32[1024,512]{1,0:T(8,128)}) fusion(f32[128,8,4,128]{3,2,1,0:T(4,128)S(1)} %bitcast.30, bf16[1024,512]{1,0:T(8,128)(2,1)S(1)} %copy-done), kind=kLoop, calls=%fused_computation.49 | loop fusion | flops 1572864 | bytes 6291456 | tf_op jit(solution)/shard_map/convert_element_type | solution.py:548
  61.7 77.5 %spread_panels.1 = (bf16[1024,512]{1,0:T(8,128)(2,1)}, bf16[512,512]{1,0:T(8,128)(2,1)}, bf16[512,512]{1,0:T(8,128)(2,1)}, bf16[512,512]{1,0:T(8,128)(2,1)}, f32[512,512]{1,0:T(8,128)}) custom-call(bf16[1024,512]{1,0:T(8,128)(2,1)} %get-tuple-element.15.front), custom_call_target="tpu_custom_call" | custom-call | tf_op jit(solution)/shard_map/spread_panels/pallas_call | solution.py:301
  139.1 11.9 %apply_update.1 = f32[1024,512]{1,0:T(8,128)} custom-call(bf16[512,512]{1,0:T(8,128)(2,1)} %get-tuple-element.10.inv_high, bf16[512,512]{1,0:T(8,128)(2,1)} %get-tuple-element.11.inv_low, f32[512,512]{1,0:T(8,128)} %get-tuple-element.12.lower, bf16[512,512]{1,0:T(8,128)(2,1)} %get-tuple-element.13.top, bf16[1024,512]{1,0:T(8,128)(2,1)} %get-tuple-element.14.panel, ...), custom_call_target="tpu_custom_call" | custom-call | tf_op jit(solution)/shard_map/apply_update/pallas_call | solution.py:493
  (5 shorter events, 0.1 us)
Async XLA Ops:
  4.5 4.7 %copy-start.1 = (s32[4,64]{1,0:T(4,128)S(1)}, s32[4,64]{1,0:T(4,128)}, u32[]{:S(2)}) copy-start(s32[4,64]{1,0:T(4,128)} %param.5) | copy-start | bytes 3076
  4.6 49.9 %all-to-all-start = ((bf16[4,4,512,128]{3,1,2,0:T(4,128)(2,1)}), bf16[4,4,512,128]{3,1,2,0:T(4,128)(2,1)S(1)}, u32[]{:S(2)}, u32[]{:S(2)}) async-start(bf16[4,4,512,128]{3,1,2,0:T(4,128)(2,1)} %convolution_convert_fusion), calls=%async_computation | async-start | bytes 4194304 | tf_op jit(solution)/shard_map/all_to_all | solution.py:541
  58.2 1.4 copy-start

commit v5 on v4

--- a/solution.py
+++ b/solution.py
@@ -42,12 +42,12 @@
     n_row,
     n_col,
     front,
+    lead,
     panel,
     top,
     inv_high,
     inv_low,
     lower,
-    lead,
     work,
     inverse,
     block_inv,
@@ -62,10 +62,6 @@
     panel_far,
     ring_right,
     ring_left,
-    lead_sub,
-    lead_col,
-    lead_gather,
-    lead_recv,
 ):
     s, r, c = lax.axis_index("sub"), lax.axis_index("row"), lax.axis_index("col")
     p = s * n_col + c
@@ -77,9 +73,6 @@
 
     def top_piece(j):
         return top.at[pl.ds(pl.multiple_of(j * PIECE, PIECE), PIECE)]
-
-    def lead_piece(j):
-        return lead.at[pl.ds(pl.multiple_of(j * PIECE, PIECE), PIECE)]
 
     def panel_piece(q):
         return panel.at[pl.ds(pl.multiple_of(q * depth, depth), depth)]
@@ -154,21 +147,8 @@
     top_share = lambda j: remote(
         top_piece(i), top_piece(i), top_gather.at[j], top_recv.at[i], at_group(j)
     )
-    lead_down = lambda k: remote(
-        top_piece(i), lead_piece(i), lead_sub.at[k], lead_recv.at[i], (k, r, 0)
-    )
-    lead_along = lambda k: remote(
-        top_piece(i), lead_piece(i), lead_col.at[k], lead_recv.at[i], (s, r, k)
-    )
-    lead_forward = lambda k: remote(
-        lead_piece(i), lead_piece(i), lead_col.at[k], lead_recv.at[i], (s, r, k)
-    )
-    lead_share = lambda j: remote(
-        lead_piece(i), lead_piece(i), lead_gather.at[j], lead_recv.at[i], at_group(j)
-    )
     own_top = pltpu.make_async_copy(front.at[pl.ds(0, WIDTH)], top, local_sem.at[0])
     own_panel = pltpu.make_async_copy(front, panel, local_sem.at[1])
-    own_lead = pltpu.make_async_copy(top, lead, local_sem.at[2])
 
     def arrived(piece, sem):
         pltpu.make_async_copy(piece, piece, sem).wait()
@@ -192,62 +172,37 @@
 
     @pl.when(p == 0)
     def _():
-        @pl.when(half != 0)
-        def _():
-            arrived(top_piece(i), top_recv.at[i])
-
-        each(n_sub, 0, lambda k: lead_down(k).start())
-        each(n_col, 0, lambda k: lead_along(k).start())
         own_panel.start()
         each(n_sub, 0, lambda k: root_down(k).start())
         for k in sorted(range(1, n_col), key=lambda k: -min(k, n_col - k)):
             panel_along(k).start()
-        share_top()
         own_panel.wait()
 
-    @pl.when(p != 0)
-    def _():
-        arrived(lead_piece(i), lead_recv.at[i])
-
-        @pl.when(c == 0)
-        def _():
-            each(n_col, 0, lambda k: lead_forward(k).start())
-
-        each(GROUP, i, lambda j: lead_share(j).start())
-
-        @pl.when(half != 0)
-        def _():
-            arrived(top_piece(i), top_recv.at[i])
-
-        share_top()
-
-        @pl.when(s == 0)
+    pl.when(half == 0)(share_top)
+
+    def pass_down():
+        @pl.when((s == 0) & (c != 0))
         def _():
             arrived(panel_piece(c), panel_recv.at[c])
             each(n_sub, 0, lambda k: panel_down(k).start())
 
-    def all_of_top():
+        @pl.when(half != 0)
+        def _():
+            arrived(top_piece(i), top_recv.at[i])
+            share_top()
+
+    def between(kb):
+        pl.when(kb == 1)(pass_down)
+        for t in range(1, last - 1):
+            pl.when(kb == t + 1)(functools.partial(ring_step, t))
+
+    factor_leading(lead, work, inverse, lower, block_inv, inv_high, inv_low, between)
+    ring_step(last - 1)
+    ring_step(last)
+
+    @pl.when(r != 0)
+    def _():
         each(GROUP, i, lambda j: arrived(top_piece(j), top_recv.at[j]))
-
-    pl.when((r != 0) & (p == 0))(all_of_top)
-
-    @pl.when(p == 0)
-    def _():
-        own_lead.start()
-        own_lead.wait()
-
-    @pl.when(p != 0)
-    def _():
-        each(GROUP, i, lambda j: arrived(lead_piece(j), lead_recv.at[j]))
-
-    def between(kb):
-        for t in range(1, last):
-            pl.when(kb == t)(functools.partial(ring_step, t))
-
-    factor_leading(lead, work, inverse, lower, block_inv, inv_high, inv_low, between)
-    ring_step(last)
-
-    pl.when((r != 0) & (p != 0))(all_of_top)
 
     @pl.when(p != 0)
     def _():
@@ -273,20 +228,10 @@
     def _():
         each(n_sub, 0, lambda k: root_down(k).wait_send())
         each(n_col, 0, lambda k: panel_along(k).wait_send())
-        each(n_sub, 0, lambda k: lead_down(k).wait_send())
-        each(n_col, 0, lambda k: lead_along(k).wait_send())
-
-    @pl.when(p != 0)
-    def _():
-        @pl.when(s == 0)
-        def _():
-            each(n_sub, 0, lambda k: panel_down(k).wait_send())
-
-        @pl.when(c == 0)
-        def _():
-            each(n_col, 0, lambda k: lead_forward(k).wait_send())
-
-        each(GROUP, i, lambda j: lead_share(j).wait_send())
+
+    @pl.when((p != 0) & (s == 0))
+    def _():
+        each(n_sub, 0, lambda k: panel_down(k).wait_send())
 
     for t in range(1, last + 1):
         go_right, go_left = ring_copies(t)
@@ -294,7 +239,7 @@
         pl.when(to_left)(go_left.wait_send)
 
 
-def spread_panels(front16, n_sub, n_row, n_col):
+def spread_panels(front16, lead, n_sub, n_row, n_col):
     rows, width = front16.shape
     vmem = pl.BlockSpec(memory_space=pltpu.VMEM)
     dma = pltpu.SemaphoreType.DMA
@@ -307,14 +252,13 @@
             jax.ShapeDtypeStruct((WIDTH, WIDTH), jnp.bfloat16),
             jax.ShapeDtypeStruct((WIDTH, WIDTH), jnp.float32),
         ),
-        in_specs=[vmem],
+        in_specs=[vmem, vmem],
         out_specs=(vmem,) * 5,
         scratch_shapes=[
-            pltpu.VMEM((WIDTH, WIDTH), jnp.bfloat16),
             pltpu.VMEM((WIDTH, WIDTH), jnp.float32),
             pltpu.VMEM((WIDTH, WIDTH), jnp.float32),
             pltpu.VMEM((TILE, TILE), jnp.float32),
-            dma((3,)),
+            dma((2,)),
             dma((GROUP,)),
             dma(()),
             dma((GROUP,)),
@@ -325,14 +269,174 @@
             dma(()),
             dma((n_col,)),
             dma((n_col,)),
+        ],
+        compiler_params=pltpu.CompilerParams(collective_id=0, has_side_effects=True),
+        name="spread_panels",
+    )(front16, lead)
+
+
+def lead_kernel(
+    n_sub,
+    n_row,
+    n_col,
+    contribution,
+    parent,
+    lead,
+    raw,
+    local_sem,
+    raw_send,
+    parent_send,
+    cross_send,
+    parent_cross,
+    raw_recv,
+    half_send,
+    col_send,
+    share_send,
+    lead_recv,
+):
+    s, r, c = lax.axis_index("sub"), lax.axis_index("row"), lax.axis_index("col")
+    half, i = r // GROUP, r % GROUP
+    across = (s, (1 - half) * GROUP + i, c)
+
+    def at_group(j):
+        return (s, half * GROUP + j, c)
+
+    def rows_of(ref, j):
+        return ref.at[pl.ds(pl.multiple_of(j * PIECE, PIECE), PIECE)]
+
+    barrier = pltpu.get_barrier_semaphore()
+
+    def greet(device):
+        pl.semaphore_signal(barrier, inc=1, device_id=device, device_id_type=MESH)
+
+    each(n_sub, s, lambda k: greet((k, r, c)))
+    each(n_col, c, lambda k: greet((s, r, k)))
+    each(GROUP, i, lambda j: greet(at_group(j)))
+    greet(across)
+    pl.semaphore_wait(barrier, n_sub - 1 + n_col - 1 + GROUP - 1 + 1)
+
+    def arrived(piece, sem):
+        pltpu.make_async_copy(piece, piece, sem).wait()
+
+    scatter = lambda j: remote(
+        rows_of(contribution, j), raw.at[s], raw_send.at[j], raw_recv.at[s], at_group(j)
+    )
+    scatter_parent = lambda j: remote(
+        rows_of(parent, j), raw.at[n_sub], parent_send.at[j], raw_recv.at[n_sub], at_group(j)
+    )
+    exchange = lambda k: remote(raw.at[s], raw.at[s], cross_send.at[k], raw_recv.at[s], (k, r, c))
+    exchange_parent = lambda k: remote(
+        raw.at[n_sub], raw.at[n_sub], parent_cross.at[k], raw_recv.at[n_sub], (k, r, c)
+    )
+    own = pltpu.make_async_copy(rows_of(contribution, 0), raw.at[s], local_sem.at[0])
+    own_parent = pltpu.make_async_copy(rows_of(parent, 0), raw.at[n_sub], local_sem.at[1])
+    mine = rows_of(lead, i)
+    over = remote(mine, mine, half_send, lead_recv.at[i], across)
+    along = lambda k: remote(mine, mine, col_send.at[k], lead_recv.at[i], (s, r, k))
+    share = lambda j: remote(mine, mine, share_send.at[j], lead_recv.at[i], at_group(j))
+    adds = (c == 0) & (half == 0)
+    first = (c == 0) & (r == 0)
+
+    @pl.when(first)
+    def _():
+        own.start()
+        each(GROUP, 0, lambda j: scatter(j).start())
+
+        @pl.when(s == 0)
+        def _():
+            own_parent.start()
+            each(GROUP, 0, lambda j: scatter_parent(j).start())
+            own_parent.wait()
+
+        own.wait()
+
+    @pl.when(adds & (r != 0))
+    def _():
+        arrived(raw.at[s], raw_recv.at[s])
+
+        @pl.when(s == 0)
+        def _():
+            arrived(raw.at[n_sub], raw_recv.at[n_sub])
+
+    @pl.when(adds)
+    def _():
+        each(n_sub, s, lambda k: exchange(k).start())
+
+        @pl.when(s == 0)
+        def _():
+            each(n_sub, 0, lambda k: exchange_parent(k).start())
+
+        each(n_sub, s, lambda k: arrived(raw.at[k], raw_recv.at[k]))
+
+        @pl.when(s != 0)
+        def _():
+            arrived(raw.at[n_sub], raw_recv.at[n_sub])
+
+        total = raw[n_sub].astype(jnp.float32)
+        for k in range(n_sub):
+            total = total + raw[k].astype(jnp.float32)
+        lead[pl.ds(pl.multiple_of(i * PIECE, PIECE), PIECE), :] = total.astype(jnp.bfloat16)
+        each(n_sub, s, lambda k: exchange(k).wait_send())
+
+        @pl.when(s == 0)
+        def _():
+            each(n_sub, 0, lambda k: exchange_parent(k).wait_send())
+
+        over.start()
+
+    @pl.when(jnp.logical_not(adds))
+    def _():
+        arrived(mine, lead_recv.at[i])
+
+    @pl.when(c == 0)
+    def _():
+        each(n_col, 0, lambda k: along(k).start())
+
+    each(GROUP, i, lambda j: share(j).start())
+    each(GROUP, i, lambda j: arrived(rows_of(lead, j), lead_recv.at[j]))
+
+    @pl.when(first)
+    def _():
+        each(GROUP, 0, lambda j: scatter(j).wait_send())
+
+        @pl.when(s == 0)
+        def _():
+            each(GROUP, 0, lambda j: scatter_parent(j).wait_send())
+
+    pl.when(adds)(over.wait_send)
+
+    @pl.when(c == 0)
+    def _():
+        each(n_col, 0, lambda k: along(k).wait_send())
+
+    each(GROUP, i, lambda j: share(j).wait_send())
+
+
+def spread_leading(contribution, parent, n_sub, n_row, n_col):
+    vmem = pl.BlockSpec(memory_space=pltpu.VMEM)
+    dma = pltpu.SemaphoreType.DMA
+    return pl.pallas_call(
+        functools.partial(lead_kernel, n_sub, n_row, n_col),
+        out_shape=jax.ShapeDtypeStruct((WIDTH, WIDTH), jnp.bfloat16),
+        in_specs=[vmem, vmem],
+        out_specs=vmem,
+        scratch_shapes=[
+            pltpu.VMEM((n_sub + 1, PIECE, WIDTH), jnp.bfloat16),
+            dma((2,)),
+            dma((GROUP,)),
+            dma((GROUP,)),
             dma((n_sub,)),
+            dma((n_sub,)),
+            dma((n_sub + 1,)),
+            dma(()),
             dma((n_col,)),
             dma((GROUP,)),
             dma((GROUP,)),
         ],
-        compiler_params=pltpu.CompilerParams(collective_id=0, has_side_effects=True),
-        name="spread_panels",
-    )(front16)
+        cost_estimate=pl.CostEstimate(flops=0, bytes_accessed=40_000_000, transcendentals=0),
+        compiler_params=pltpu.CompilerParams(collective_id=1, has_side_effects=True),
+        name="spread_leading",
+    )(contribution, parent)
 
 
 def invert_block(block, store_rows):
@@ -538,6 +642,16 @@
         local_row[:, :, None] == jnp.arange(front_rows, dtype=jnp.int32)[None, None, :]
     )
     place_row = row_hit.astype(jnp.bfloat16)
+    own_place = lax.dynamic_index_in_dim(place_row, sub_id, 0, keepdims=False)[:, :panel_tiles]
+    own_grid = payload[0].reshape(panel_tiles, child_rows, tile_len, tile_len)
+    contribution = (
+        jnp.einsum("ka,qkyx->ayqx", own_place, own_grid, preferred_element_type=jnp.float32)
+        .astype(jnp.bfloat16)
+        .reshape(WIDTH, WIDTH)
+    )
+    lead = spread_leading(
+        contribution, parent_front[:WIDTH], sub_count, row_count, col_count
+    )
     arrived = lax.all_to_all(payload, "sub", split_axis=0, concat_axis=0, tiled=True)
     slot_count = arrived.shape[1]
     grid = arrived.reshape(sub_count, slot_count, child_rows, tile_len, tile_len)
@@ -545,7 +659,7 @@
     placed = spread.reshape(front_rows * tile_len, slot_count * tile_len)
     front_local = parent_front.astype(jnp.float32) + placed
     panel, top, inv_high, inv_low, lower = spread_panels(
-        front_local.astype(jnp.bfloat16), sub_count, row_count, col_count
+        front_local.astype(jnp.bfloat16), lead, sub_count, row_count, col_count
     )
     return apply_update(inv_high, inv_low, lower, top, panel, front_local)
 

time: 153 us -> 159 us (1.039)
  the two profiles are of different devices: /device:TPU:449 before, /device:TPU:84 now
where the time goes in v5:
time: 159 us
  Pallas kernels  134 us (84%)
  local copies, waits for them, and re-layouts  8.22 us (5%)
  matrix products  7.4 us (5%)
  starting transfers between devices  7.04 us (4%)
  other arithmetic  2.27 us (1%)
    pallas_call x1, Pallas kernels, spread_panels(): pl.pallas_call(functools.partial(spread_kernel, n_sub, n_row, n_col), out...  64.8 us
    pallas_call x1, Pallas kernels, spread_leading(): pl.pallas_call(functools.partial(lead_kernel, n_sub, n_row, n_col), out_s...  57.1 us
    pallas_call x1, Pallas kernels, apply_update(): pl.pallas_call(update_kernel, out_shape=jax.ShapeDtypeStruct(front.shape,...  11.8 us
    all_to_all x1, starting transfers between devices, body(): lax.all_to_all(payload, 'sub', split_axis=0, concat_axis=0, tiled=True)  7.04 us
    dot_general x1, matrix products, body(): jnp.einsum('ska,sqkyx->ayqx', place_row, grid, preferred_element_type=jnp...  3.55 us
  transfers between devices with their start and end apart: 1, of which 0 were waited for; matrix products, arithmetic and copies ran while one was open for 4% of the time, Pallas kernels for 36%

profile of v5, /device:TPU:84, one launch (start us, length us, event | category | flops | bytes accessed | tf_op | source)
XLA Modules:
  0.0 158.8 jit_solution(11418031292189999178)
XLA Ops:
  0.0 0.7 fusion.22
  0.7 0.1 reshape.141
  0.8 0.2 dynamic-slice_reduce_fusion
  1.0 1.5 copy.27
  2.5 2.0 %convolution_convert_fusion = bf16[4,4,512,128]{3,1,2,0:T(4,128)(2,1)} fusion(bf16[512,8,128,1]{2,1,0,3:T(8,128)(2,1)S(1)} %bitcast.45, pred[4,8]{1,0:T(4,128)(4,1)S(1)} %get-tuple-element.19, pred[4,8]{1,0:T(4,128)(4,1)S(1)} %get-tuple-element.20), kind=kOutput, calls=%fused_computation.3 | convolution fusion | flops 17825920 | bytes 3145792 | tf_op jit(solution)/shard_map/dqk,rky->dqry/dot_general | solution.py:632
  4.5 0.0 copy-start.1
  4.6 0.0 copy-start
  4.6 7.0 %all-to-all-start = ((bf16[4,4,512,128]{3,1,2,0:T(4,128)(2,1)}), bf16[4,4,512,128]{3,1,2,0:T(4,128)(2,1)S(1)}, u32[]{:S(2)}, u32[]{:S(2)}) async-start(bf16[4,4,512,128]{3,1,2,0:T(4,128)(2,1)} %convolution_convert_fusion), calls=%async_computation | async-start | bytes 4194304 | tf_op jit(solution)/shard_map/all_to_all | solution.py:655
  11.6 0.0 copy-done.1
  11.6 0.1 reshape.144
  11.7 2.0 %slice.12 = bf16[1,4,512,128]{3,1,2,0:T(4,128)(2,1)} slice(bf16[4,4,512,128]{3,1,2,0:T(4,128)(2,1)} %convolution_convert_fusion), slice={[0:1], [0:4], [0:512], [0:128]} | slice | bytes 1048576 | tf_op jit(solution)/shard_map/slice | solution.py:646
  13.7 0.1 constant_dynamic-slice_fusion
  13.8 0.1 copy.25
  13.9 0.0 copy-done
  13.9 0.8 slice.11.parent
  14.7 0.1 fusion.7
  14.8 1.8 %fusion.5 = bf16[4,128,4,128]{3,0,1,2:T(4,128)(2,1)S(1)} fusion(bf16[4,4,128,128]{3,0,2,1:T(4,128)(2,1)} %bitcast.50, pred[4,8]{1,0:T(4,128)(4,1)S(1)} %dynamic-slice_bitcast_fusion), kind=kOutput, calls=%fused_computation.6 | convolution fusion | flops 2359296 | bytes 1048608 | tf_op jit(solution)/shard_map/ka,qkyx->ayqx/dot_general | solution.py:648
  16.7 0.4 copy.17
  17.1 0.9 copy.39
  17.9 57.1 %spread_leading.1.lead = bf16[512,512]{1,0:T(8,128)(2,1)} custom-call(bf16[512,512]{1,0:T(8,128)(2,1)} %bitcast.46, bf16[512,512]{1,0:T(8,128)(2,1)} %slice.11.parent), custom_call_target="tpu_custom_call" | custom-call | bytes 40000000 | tf_op jit(solution)/shard_map/spread_leading/pallas_call | solution.py:418
  75.1 0.0 all-to-all-done
  75.1 3.5 %fusion.2 = f32[8,128,4,128]{3,0,1,2:T(8,128)S(1)} fusion(bf16[4,4,4,128,128]{4,1,3,2,0:T(4,128)(2,1)S(1)} %bitcast.47, pred[4,4,8]{2,1,0:T(4,128)(4,1)S(1)} %fusion.7), kind=kOutput, calls=%fused_computation.4 | convolution fusion | flops 16777216 | bytes 4194432 | tf_op jit(solution)/shard_map/ska,sqkyx->ayqx/dot_general | solution.py:658
  78.6 1.4 copy.14
  80.0 2.1 %fusion.23 = (bf16[1024,512]{1,0:T(8,128)(2,1)}, f32[1024,512]{1,0:T(8,128)}) fusion(f32[128,8,4,128]{3,2,1,0:T(4,128)S(1)} %bitcast.44, bf16[1024,512]{1,0:T(8,128)(2,1)S(1)} %copy-done), kind=kLoop, calls=%fused_computation.54 | loop fusion | flops 1572864 | bytes 6291456 | tf_op jit(solution)/shard_map/convert_element_type | solution.py:662
  82.1 64.8 %spread_panels.1 = (bf16[1024,512]{1,0:T(8,128)(2,1)}, bf16[512,512]{1,0:T(8,128)(2,1)}, bf16[512,512]{1,0:T(8,128)(2,1)}, bf16[512,512]{1,0:T(8,128)(2,1)}, f32[512,512]{1,0:T(8,128)}) custom-call(bf16[1024,512]{1,0:T(8,128)(2,1)} %get-tuple-element.15.front, bf16[512,512]{1,0:T(8,128)(2,1)} %spread_leading.1.lead), custom_call_target="tpu_custom_call" | custom-call | tf_op jit(solution)/shard_map/spread_panels/pallas_call | solution.py:246
  146.9 11.8 %apply_update.1 = f32[1024,512]{1,0:T(8,128)} custom-call(bf16[512,512]{1,0:T(8,128)(2,1)} %get-tuple-element.10.inv_high, bf16[512,512]{1,0:T(8,128)(2,1)} %get-tuple-element.11.inv_low, f32[512,512]{1,0:T(8,128)} %get-tuple-element.12.lower, bf16[512,512]{1,0:T(8,128)(2,1)} %get-tuple-element.13.top, bf16[1024,512]{1,0:T(8,128)(2,1)} %get-tuple-element.14.panel, ...), custom_call_target="tpu_custom_call" | custom-call | tf_op jit(solution)/shard_map/apply_update/pallas_call | solution.py:597
  (6 shorter events, 0.1 us)
Async XLA Ops:
  4.5 7.0 %copy-start.1 = (s32[4,64]{1,0:T(4,128)S(1)}, s32[4,64]{1,0:T(4,128)}, u32[]{:S(2)}) copy-start(s32[4,64]{1,0:T(4,128)} %param.5) | copy-start | bytes 3076
  4.6 9.3 %copy-start = (bf16[1024,512]{1,0:T(8,128)(2,1)S(1)}, bf16[1024,512]{1,0:T(8,128)(2,1)}, u32[]{:S(2)}) copy-start(bf16[1024,512]{1,0:T(8,128)(2,1)} %param.4) | copy-start | bytes 3145732
  4.6 70.5 %all-to-all-start = ((bf16[4,4,512,128]{3,1,2,0:T(4,128)(2,1)}), bf16[4,4,512,128]{3,1,2,0:T(4,128)(2,1)S(1)}, u32[]{:S(2)}, u32[]{:S(2)}) async-start(bf16[4,4,512,128]{3,1,2,0:T(4,128)(2,1)} %convolution_convert_fusion), calls=%async_computation | async-start | bytes 4194304 | tf_op jit(solution)/shard_map/all_to_all | solution.py:655

commit v6 on v4

--- a/solution.py
+++ b/solution.py
@@ -35,6 +35,10 @@
         return 0
 
     lax.fori_loop(0, count, step, 0)
+
+
+def farthest_first(count):
+    return sorted(range(1, count), key=lambda k: -min(k, count - k))
 
 
 def spread_kernel(
@@ -197,10 +201,11 @@
             arrived(top_piece(i), top_recv.at[i])
 
         each(n_sub, 0, lambda k: lead_down(k).start())
-        each(n_col, 0, lambda k: lead_along(k).start())
+        for k in farthest_first(n_col):
+            lead_along(k).start()
         own_panel.start()
         each(n_sub, 0, lambda k: root_down(k).start())
-        for k in sorted(range(1, n_col), key=lambda k: -min(k, n_col - k)):
+        for k in farthest_first(n_col):
             panel_along(k).start()
         share_top()
         own_panel.wait()
@@ -211,15 +216,11 @@
 
         @pl.when(c == 0)
         def _():
-            each(n_col, 0, lambda k: lead_forward(k).start())
-
-        each(GROUP, i, lambda j: lead_share(j).start())
-
-        @pl.when(half != 0)
-        def _():
-            arrived(top_piece(i), top_recv.at[i])
-
-        share_top()
+            for k in farthest_first(n_col):
+                lead_forward(k).start()
+
+        for k in farthest_first(GROUP):
+            lead_share((i + k) % GROUP).start()
 
         @pl.when(s == 0)
         def _():
@@ -240,12 +241,24 @@
     def _():
         each(GROUP, i, lambda j: arrived(lead_piece(j), lead_recv.at[j]))
 
-    def between(kb):
-        for t in range(1, last):
-            pl.when(kb == t)(functools.partial(ring_step, t))
+    def pass_top():
+        @pl.when(p != 0)
+        def _():
+            @pl.when(half != 0)
+            def _():
+                arrived(top_piece(i), top_recv.at[i])
+
+            share_top()
+
+    def between(kb, late):
+        if late:
+            for t in range(1, last):
+                pl.when(kb == t)(functools.partial(ring_step, t + 1))
+        else:
+            pl.when(kb == 0)(pass_top)
+            pl.when(kb == 1)(functools.partial(ring_step, 1))
 
     factor_leading(lead, work, inverse, lower, block_inv, inv_high, inv_low, between)
-    ring_step(last)
 
     pl.when((r != 0) & (p != 0))(all_of_top)
 
@@ -433,10 +446,11 @@
             block_inv[j0 + k : j0 + k + 1, :] = x[k][0:1, :]
 
     def step(kb, _):
-        between(kb)
+        between(kb, False)
         o = pl.multiple_of(kb * TILE, TILE)
         here = pl.ds(o, TILE)
         invert_block(work[here, here], store_rows)
+        between(kb, True)
         d_inv = block_inv[...]
         below = mul3(work[:, here], d_inv, True)
         line = lax.broadcasted_iota(jnp.int32, (width, TILE), 0)

time: 153 us -> 151 us (0.987); the launches traced: 151 us -> 151 us
  no operation moved by 1% of the time
where the time goes in v6:
time: 151 us
  Pallas kernels  89.4 us (59%)
  waiting for transfers between devices  44.7 us (30%)
  matrix products  5.72 us (4%)
  starting transfers between devices  4.66 us (3%)
  local copies, waits for them, and re-layouts  4.29 us (3%)
  other arithmetic  2.19 us (1%)
    pallas_call x1, Pallas kernels, spread_panels(): pl.pallas_call(functools.partial(spread_kernel, n_sub, n_row, n_col), out...  77.6 us
    all_to_all x1, waiting for transfers between devices, body(): lax.all_to_all(payload, 'sub', split_axis=0, concat_axis=0, tiled=True)  44.7 us
    pallas_call x1, Pallas kernels, apply_update(): pl.pallas_call(update_kernel, out_shape=jax.ShapeDtypeStruct(front.shape,...  11.8 us
    all_to_all x1, starting transfers between devices, body(): lax.all_to_all(payload, 'sub', split_axis=0, concat_axis=0, tiled=True)  4.66 us
    dot_general x1, matrix products, body(): jnp.einsum('ska,sqkyx->ayqx', place_row, grid, preferred_element_type=jnp...  3.69 us
  transfers between devices with their start and end apart: 1, of which 1 were waited for; matrix products, arithmetic and copies ran while one was open for 0% of the time, Pallas kernels for 0%

profile of v6, /device:TPU:449, one launch (start us, length us, event | category | flops | bytes accessed | tf_op | source)
XLA Modules:
  0.0 151.1 jit_solution(9681512691184112677)
XLA Ops:
  0.0 0.7 fusion.21
  0.7 0.1 reshape.138
  0.8 0.2 dynamic-slice_reduce_fusion
  1.0 1.5 copy.18
  2.5 2.0 %convolution_convert_fusion = bf16[4,4,512,128]{3,1,2,0:T(4,128)(2,1)} fusion(bf16[512,8,128,1]{2,1,0,3:T(8,128)(2,1)S(1)} %bitcast.31, pred[4,8]{1,0:T(4,128)(4,1)S(1)} %get-tuple-element.19, pred[4,8]{1,0:T(4,128)(4,1)S(1)} %get-tuple-element.20), kind=kOutput, calls=%fused_computation.3 | convolution fusion | flops 17825920 | bytes 3145792 | tf_op jit(solution)/shard_map/dqk,rky->dqry/dot_general | solution.py:542
  4.5 0.0 copy-start.1
  4.6 4.7 %all-to-all-start = ((bf16[4,4,512,128]{3,1,2,0:T(4,128)(2,1)}), bf16[4,4,512,128]{3,1,2,0:T(4,128)(2,1)S(1)}, u32[]{:S(2)}, u32[]{:S(2)}) async-start(bf16[4,4,512,128]{3,1,2,0:T(4,128)(2,1)} %convolution_convert_fusion), calls=%async_computation | async-start | bytes 4194304 | tf_op jit(solution)/shard_map/all_to_all | solution.py:555
  9.2 0.0 copy-done.1
  9.2 0.1 reshape.141
  9.3 0.1 constant_dynamic-slice_fusion
  9.4 0.1 copy.17
  9.5 0.1 copy.11
  9.6 0.1 copy.10
  9.7 44.7 %all-to-all-done = bf16[4,4,512,128]{3,1,2,0:T(4,128)(2,1)S(1)} async-done(((bf16[4,4,512,128]{3,1,2,0:T(4,128)(2,1)}), bf16[4,4,512,128]{3,1,2,0:T(4,128)(2,1)S(1)}, u32[]{:S(2)}, u32[]{:S(2)}) %all-to-all-start) | async-done | bytes 2097184 | tf_op jit(solution)/shard_map/all_to_all | solution.py:555
  54.5 3.7 %fusion.2 = f32[8,128,4,128]{3,0,1,2:T(8,128)S(1)} fusion(bf16[4,4,4,128,128]{4,1,3,2,0:T(4,128)(2,1)S(1)} %bitcast.32, s32[4,4]{0,1:T(4,128)S(1)} %copy.11, pred[4,4]{0,1:T(4,128)(4,1)S(1)} %copy.10), kind=kOutput, calls=%fused_computation.4 | convolution fusion | flops 16777472 | bytes 4194384 | tf_op jit(solution)/shard_map/ska,sqkyx->ayqx/dot_general | solution.py:558
  58.2 0.0 copy-start
  58.2 1.4 copy.13
  59.5 0.0 copy-done
  59.5 2.1 %fusion.22 = (bf16[1024,512]{1,0:T(8,128)(2,1)}, f32[1024,512]{1,0:T(8,128)}) fusion(f32[128,8,4,128]{3,2,1,0:T(4,128)S(1)} %bitcast.30, bf16[1024,512]{1,0:T(8,128)(2,1)S(1)} %copy-done), kind=kLoop, calls=%fused_computation.49 | loop fusion | flops 1572864 | bytes 6291456 | tf_op jit(solution)/shard_map/convert_element_type | solution.py:562
  61.7 77.6 %spread_panels.1 = (bf16[1024,512]{1,0:T(8,128)(2,1)}, bf16[512,512]{1,0:T(8,128)(2,1)}, bf16[512,512]{1,0:T(8,128)(2,1)}, bf16[512,512]{1,0:T(8,128)(2,1)}, f32[512,512]{1,0:T(8,128)}) custom-call(bf16[1024,512]{1,0:T(8,128)(2,1)} %get-tuple-element.15.front), custom_call_target="tpu_custom_call" | custom-call | tf_op jit(solution)/shard_map/spread_panels/pallas_call | solution.py:314
  139.2 11.8 %apply_update.1 = f32[1024,512]{1,0:T(8,128)} custom-call(bf16[512,512]{1,0:T(8,128)(2,1)} %get-tuple-element.10.inv_high, bf16[512,512]{1,0:T(8,128)(2,1)} %get-tuple-element.11.inv_low, f32[512,512]{1,0:T(8,128)} %get-tuple-element.12.lower, bf16[512,512]{1,0:T(8,128)(2,1)} %get-tuple-element.13.top, bf16[1024,512]{1,0:T(8,128)(2,1)} %get-tuple-element.14.panel, ...), custom_call_target="tpu_custom_call" | custom-call | tf_op jit(solution)/shard_map/apply_update/pallas_call | solution.py:507
  (5 shorter events, 0.1 us)
Async XLA Ops:
  4.5 4.7 %copy-start.1 = (s32[4,64]{1,0:T(4,128)S(1)}, s32[4,64]{1,0:T(4,128)}, u32[]{:S(2)}) copy-start(s32[4,64]{1,0:T(4,128)} %param.5) | copy-start | bytes 3076
  4.6 49.9 %all-to-all-start = ((bf16[4,4,512,128]{3,1,2,0:T(4,128)(2,1)}), bf16[4,4,512,128]{3,1,2,0:T(4,128)(2,1)S(1)}, u32[]{:S(2)}, u32[]{:S(2)}) async-start(bf16[4,4,512,128]{3,1,2,0:T(4,128)(2,1)} %convolution_convert_fusion), calls=%async_computation | async-start | bytes 4194304 | tf_op jit(solution)/shard_map/all_to_all | solution.py:555
  58.2 1.4 copy-start

commit v7 on v6

--- a/solution.py
+++ b/solution.py
@@ -469,12 +469,14 @@
     inv_low[...] = low
 
 
-def update_kernel(inv_high, inv_low, lower, top, panel, front, out, right):
+def update_kernel(inv_high, inv_low, lower, top, panel, front, out, right_high, right_low):
     row_id = lax.axis_index("row")
     block_id = lax.axis_index("sub") * lax.axis_size("col") + lax.axis_index("col")
     tops = top[...]
-    right[...] = mul(inv_high[...], tops) + mul(inv_low[...], tops)
-    chunk = 128
+    high, low = split(mul(inv_high[...], tops) + mul(inv_low[...], tops))
+    right_high[...] = high
+    right_low[...] = low
+    chunk = 256
 
     @pl.loop(0, panel.shape[0] // chunk)
     def _(t):
@@ -499,7 +501,11 @@
 
             @pl.when(jnp.logical_not(head))
             def _():
-                out[rows, :] = front[rows, :] - mul3(f_rows, right[...])
+                fh, fl = split(f_rows)
+                out[rows, :] = front[rows, :] - (
+                    mul(fh, right_high[...])
+                    + (mul(fh, right_low[...]) + mul(fl, right_high[...]))
+                )
 
 
 def apply_update(inv_high, inv_low, lower, top, panel, front):
@@ -509,7 +515,7 @@
         out_shape=jax.ShapeDtypeStruct(front.shape, jnp.float32),
         in_specs=[vmem] * 6,
         out_specs=vmem,
-        scratch_shapes=[pltpu.VMEM((WIDTH, WIDTH), jnp.float32)],
+        scratch_shapes=[pltpu.VMEM((WIDTH, WIDTH), jnp.bfloat16)] * 2,
         name="apply_update",
     )(inv_high, inv_low, lower, top, panel, front)
 

time: 151 us -> 149 us (0.987)
  Pallas kernels: 89.4 us -> 86.5 us
    pallas_call x1, Pallas kernels: 11.8 us -> 8.97 us  [apply_update(): pl.pallas_call(update_kernel, out_shape=jax.ShapeDtypeStruct(front.shape,...]
where the time goes in v7:
time: 149 us; the launch traced here: 148 us
  Pallas kernels  86.5 us (58%)
  waiting for transfers between devices  44.7 us (30%)
  matrix products  5.72 us (4%)
  starting transfers between devices  4.66 us (3%)
  local copies, waits for them, and re-layouts  4.29 us (3%)
  other arithmetic  2.19 us (1%)
    pallas_call x1, Pallas kernels, spread_panels(): pl.pallas_call(functools.partial(spread_kernel, n_sub, n_row, n_col), out...  77.6 us
    all_to_all x1, waiting for transfers between devices, body(): lax.all_to_all(payload, 'sub', split_axis=0, concat_axis=0, tiled=True)  44.7 us
    pallas_call x1, Pallas kernels, apply_update(): pl.pallas_call(update_kernel, out_shape=jax.ShapeDtypeStruct(front.shape,...  8.97 us
    all_to_all x1, starting transfers between devices, body(): lax.all_to_all(payload, 'sub', split_axis=0, concat_axis=0, tiled=True)  4.66 us
    dot_general x1, matrix products, body(): jnp.einsum('ska,sqkyx->ayqx', place_row, grid, preferred_element_type=jnp...  3.69 us
  transfers between devices with their start and end apart: 1, of which 1 were waited for; matrix products, arithmetic and copies ran while one was open for 0% of the time, Pallas kernels for 0%

profile of v7, /device:TPU:449, one launch (start us, length us, event | category | flops | bytes accessed | tf_op | source)
XLA Modules:
  0.0 148.2 jit_solution(4987443329626512851)
XLA Ops:
  0.0 0.7 fusion.21
  0.7 0.1 reshape.138
  0.8 0.2 dynamic-slice_reduce_fusion
  1.0 1.5 %copy.18 = bf16[64,8,8,128]{3,2,1,0:T(8,128)(2,1)S(1)} copy(bf16[64,8,8,128]{3,1,2,0:T(8,128)(2,1)} %bitcast.33) | data formatting | bytes 2097152
  2.5 2.0 %convolution_convert_fusion = bf16[4,4,512,128]{3,1,2,0:T(4,128)(2,1)} fusion(bf16[512,8,128,1]{2,1,0,3:T(8,128)(2,1)S(1)} %bitcast.31, pred[4,8]{1,0:T(4,128)(4,1)S(1)} %get-tuple-element.19, pred[4,8]{1,0:T(4,128)(4,1)S(1)} %get-tuple-element.20), kind=kOutput, calls=%fused_computation.3 | convolution fusion | flops 17825920 | bytes 3145792 | tf_op jit(solution)/shard_map/dqk,rky->dqry/dot_general | solution.py:548
  4.5 0.0 copy-start.1
  4.6 4.7 %all-to-all-start = ((bf16[4,4,512,128]{3,1,2,0:T(4,128)(2,1)}), bf16[4,4,512,128]{3,1,2,0:T(4,128)(2,1)S(1)}, u32[]{:S(2)}, u32[]{:S(2)}) async-start(bf16[4,4,512,128]{3,1,2,0:T(4,128)(2,1)} %convolution_convert_fusion), calls=%async_computation | async-start | bytes 4194304 | tf_op jit(solution)/shard_map/all_to_all | solution.py:561
  9.2 0.0 copy-done.1
  9.2 0.1 reshape.141
  9.3 0.1 constant_dynamic-slice_fusion
  9.4 0.1 copy.17
  9.5 0.1 copy.11
  9.6 0.1 copy.10
  9.7 44.7 %all-to-all-done = bf16[4,4,512,128]{3,1,2,0:T(4,128)(2,1)S(1)} async-done(((bf16[4,4,512,128]{3,1,2,0:T(4,128)(2,1)}), bf16[4,4,512,128]{3,1,2,0:T(4,128)(2,1)S(1)}, u32[]{:S(2)}, u32[]{:S(2)}) %all-to-all-start) | async-done | bytes 2097184 | tf_op jit(solution)/shard_map/all_to_all | solution.py:561
  54.5 3.7 %fusion.2 = f32[8,128,4,128]{3,0,1,2:T(8,128)S(1)} fusion(bf16[4,4,4,128,128]{4,1,3,2,0:T(4,128)(2,1)S(1)} %bitcast.32, s32[4,4]{0,1:T(4,128)S(1)} %copy.11, pred[4,4]{0,1:T(4,128)(4,1)S(1)} %copy.10), kind=kOutput, calls=%fused_computation.4 | convolution fusion | flops 16777472 | bytes 4194384 | tf_op jit(solution)/shard_map/ska,sqkyx->ayqx/dot_general | solution.py:564
  58.2 0.0 copy-start
  58.2 1.4 copy.13
  59.5 0.0 copy-done
  59.5 2.1 %fusion.22 = (bf16[1024,512]{1,0:T(8,128)(2,1)}, f32[1024,512]{1,0:T(8,128)}) fusion(f32[128,8,4,128]{3,2,1,0:T(4,128)S(1)} %bitcast.30, bf16[1024,512]{1,0:T(8,128)(2,1)S(1)} %copy-done), kind=kLoop, calls=%fused_computation.49 | loop fusion | flops 1572864 | bytes 6291456 | tf_op jit(solution)/shard_map/convert_element_type | solution.py:568
  61.7 77.6 %spread_panels.1 = (bf16[1024,512]{1,0:T(8,128)(2,1)}, bf16[512,512]{1,0:T(8,128)(2,1)}, bf16[512,512]{1,0:T(8,128)(2,1)}, bf16[512,512]{1,0:T(8,128)(2,1)}, f32[512,512]{1,0:T(8,128)}) custom-call(bf16[1024,512]{1,0:T(8,128)(2,1)} %get-tuple-element.15.front), custom_call_target="tpu_custom_call" | custom-call | tf_op jit(solution)/shard_map/spread_panels/pallas_call | solution.py:314
  139.2 9.0 %apply_update.1 = f32[1024,512]{1,0:T(8,128)} custom-call(bf16[512,512]{1,0:T(8,128)(2,1)} %get-tuple-element.10.inv_high, bf16[512,512]{1,0:T(8,128)(2,1)} %get-tuple-element.11.inv_low, f32[512,512]{1,0:T(8,128)} %get-tuple-element.12.lower, bf16[512,512]{1,0:T(8,128)(2,1)} %get-tuple-element.13.top, bf16[1024,512]{1,0:T(8,128)(2,1)} %get-tuple-element.14.panel, ...), custom_call_target="tpu_custom_call" | custom-call | tf_op jit(solution)/shard_map/apply_update/pallas_call | solution.py:513
  (5 shorter events, 0.1 us)
Async XLA Ops:
  4.5 4.7 %copy-start.1 = (s32[4,64]{1,0:T(4,128)S(1)}, s32[4,64]{1,0:T(4,128)}, u32[]{:S(2)}) copy-start(s32[4,64]{1,0:T(4,128)} %param.5) | copy-start | bytes 3076
  4.6 49.9 %all-to-all-start = ((bf16[4,4,512,128]{3,1,2,0:T(4,128)(2,1)}), bf16[4,4,512,128]{3,1,2,0:T(4,128)(2,1)S(1)}, u32[]{:S(2)}, u32[]{:S(2)}) async-start(bf16[4,4,512,128]{3,1,2,0:T(4,128)(2,1)} %convolution_convert_fusion), calls=%async_computation | async-start | bytes 4194304 | tf_op jit(solution)/shard_map/all_to_all | solution.py:561
  58.2 1.4 copy-start
